TPU v7x, 32 devices: a whole 2x2x4 slice. The times are simulated.
32 devices in a mesh: grp: 4 (over x, core), wf: 8 (over z, y).
Axes of the slice: x: 2, y: 2, z: 4, core: 2. Of those that a mesh axis runs over, the one named last changes fastest.
Arguments:
- quasi: float32 [32, 4, 262144], P(('grp', 'wf')), may hold values from -6 to 6
- outer_field: float32 [262144], replicated, may hold values from -4 to 4
- coupling: float32 [262144], replicated, may hold values from 2 to 16
Outputs:
- evolved: float32 [32, 4, 262144], P(('grp', 'wf'))
- potentials: float32 [3, 64, 4096], P(None, 'grp', 'wf')
All inputs are finite; a program needn't handle non-finite values.
Results may differ from a plain program's by a relative error of at most 0.0003.
Values sent between devices are 32-bit elements; how exact they have to be, the bound alone decides.
No kernel may reach another device: no remote copies, remote signals or barrier semaphores. Data moves between devices by JAX's collectives and lax.ppermute only.
A program may use at most 192 MiB of HBM per device.

v0:
```python
import math

import jax
import jax.numpy as jnp
from jax import lax
from jax.sharding import PartitionSpec as P

NX = 64
NG = 64


time_step = 0.2
kinetic_coef = 0.5
density_coef = 1.0
coulomb_coef = 0.25


def neighbour_sum(field, first, grid):
    positions = jnp.arange(first * grid * grid, dtype=jnp.int32)
    depth_index = positions % grid
    column_index = positions // grid % grid
    plane = grid * grid
    total = jnp.roll(field, plane, -1) + jnp.roll(field, -plane, -1)
    total = total + jnp.where(
        column_index == grid - 1, jnp.roll(field, (grid - 1) * grid, -1), jnp.roll(field, -grid, -1)
    )
    total = total + jnp.where(
        column_index == 0, jnp.roll(field, -(grid - 1) * grid, -1), jnp.roll(field, grid, -1)
    )
    total = total + jnp.where(
        depth_index == grid - 1, jnp.roll(field, grid - 1, -1), jnp.roll(field, -1, -1)
    )
    total = total + jnp.where(
        depth_index == 0, jnp.roll(field, 1 - grid, -1), jnp.roll(field, 1, -1)
    )
    return total - 6.0 * field


def hamiltonian(state, laplace, fields):
    mean_field, pair_real, pair_imag = (fields[0], fields[1], fields[2])
    single = -kinetic_coef * laplace + mean_field * state
    first = single[..., 0, :] + pair_real * state[..., 2, :] - pair_imag * state[..., 3, :]
    second = single[..., 1, :] + pair_real * state[..., 3, :] + pair_imag * state[..., 2, :]
    third = pair_real * state[..., 0, :] + pair_imag * state[..., 1, :] - single[..., 2, :]
    fourth = pair_real * state[..., 1, :] - pair_imag * state[..., 0, :] - single[..., 3, :]
    return jnp.stack([first, second, third, fourth], axis=-2)


def propagate(state, laplace, fields, first, grid):
    result = state
    term = state
    for degree in range(1, 5):
        current = laplace if degree == 1 else neighbour_sum(term, first, grid)
        applied = hamiltonian(term, current, fields)
        factor = time_step / degree
        term = jnp.stack(
            [
                factor * applied[..., 1, :],
                -factor * applied[..., 0, :],
                factor * applied[..., 3, :],
                -factor * applied[..., 2, :],
            ],
            axis=-2,
        )
        result = result + term
    return result


def lattice_symbol(indices, length):
    return 2.0 - 2.0 * jnp.cos(2.0 * math.pi / length * indices.astype(jnp.float32))


def coulomb_kernel(first_index, second_index, third_index, first_len, grid):
    squared = (
        lattice_symbol(first_index, first_len)[:, None, None]
        + lattice_symbol(second_index, grid)[None, :, None]
        + lattice_symbol(third_index, grid)[None, None, :]
    )
    return jnp.where(
        squared > 0.001,
        4.0 * math.pi * coulomb_coef / jnp.where(squared > 0.001, squared, 1.0),
        0.0,
    )


def transform(real_part, imag_part, axis, inverse):
    length = real_part.shape[axis]
    series = jnp.arange(length, dtype=jnp.int32)
    angle = (
        2.0 * math.pi / length * (series[:, None] * series[None, :] % length).astype(jnp.float32)
    )
    cosine = jnp.cos(angle)
    sine = jnp.sin(angle)
    moved_real = jnp.moveaxis(real_part, axis, -1)
    moved_imag = jnp.moveaxis(imag_part, axis, -1)

    def apply(matrix, values):
        return jnp.dot(values, matrix, precision=lax.Precision.HIGHEST)

    if inverse:
        new_real = (apply(cosine, moved_real) - apply(sine, moved_imag)) / length
        new_imag = (apply(cosine, moved_imag) + apply(sine, moved_real)) / length
    else:
        new_real = apply(cosine, moved_real) + apply(sine, moved_imag)
        new_imag = apply(cosine, moved_imag) - apply(sine, moved_real)
    return (jnp.moveaxis(new_real, -1, axis), jnp.moveaxis(new_imag, -1, axis))


def local(quasi, outer_field, coupling):
    grid = NG
    first_len = NX
    waves_total = quasi.shape[0] * lax.axis_size("grp") * lax.axis_size("wf")
    laplace = neighbour_sum(quasi, first_len, grid)
    partial_value = (
        jnp.stack(
            [
                jnp.sum(quasi[:, 2] * quasi[:, 2] + quasi[:, 3] * quasi[:, 3], axis=0),
                jnp.sum(quasi[:, 0] * quasi[:, 2] + quasi[:, 1] * quasi[:, 3], axis=0),
                jnp.sum(quasi[:, 1] * quasi[:, 2] - quasi[:, 0] * quasi[:, 3], axis=0),
            ]
        )
        / waves_total
    )
    rows = first_len // lax.axis_size("grp")
    width = grid * grid // lax.axis_size("wf")
    row_start = lax.axis_index("grp") * rows
    col_start = lax.axis_index("wf") * width
    summed = lax.psum(partial_value, ("grp", "wf"))
    cube = summed[0].reshape(first_len, grid, grid)
    real_part, imag_part = transform(cube, jnp.zeros_like(cube), 2, False)
    real_part, imag_part = transform(real_part, imag_part, 1, False)
    real_part, imag_part = transform(real_part, imag_part, 0, False)
    series = jnp.arange(grid, dtype=jnp.int32)
    kernel = coulomb_kernel(jnp.arange(first_len, dtype=jnp.int32), series, series, first_len, grid)
    real_part, imag_part = transform(real_part * kernel, imag_part * kernel, 0, True)
    real_part, imag_part = transform(real_part, imag_part, 1, True)
    real_part, imag_part = transform(real_part, imag_part, 2, True)
    fields = jnp.stack(
        [
            outer_field + density_coef * summed[0] + real_part.reshape(-1),
            -coupling * summed[1],
            -coupling * summed[2],
        ]
    )
    potentials = lax.dynamic_slice(
        fields.reshape(3, first_len, grid * grid), (0, row_start, col_start), (3, rows, width)
    )
    evolved = propagate(quasi, laplace, fields, first_len, grid)
    return (evolved, potentials)


def solution(mesh):
    placed = (P(("grp", "wf"), None, None), P(), P())
    return jax.shard_map(
        local,
        mesh=mesh,
        in_specs=placed,
        out_specs=(P(("grp", "wf"), None, None), P(None, "grp", "wf")),
        check_vma=False,
    )
```

profile of v0, /device:TPU:0, one launch (start us, length us, event | category | flops | bytes accessed | tf_op | source)
XLA Modules:
  0.0 596.0 jit_solution(14109147061613435823)
XLA Ops:
  7.2 13.3 %fusion.256 = (f32[1,1,262144]{2,1,0:T(1,128)}, f32[1,262144]{1,0:T(1,128)S(1)}, f32[1,262144]{1,0:T(1,128)S(1)}, f32[1,262144]{1,0:T(1,128)S(1)}, f32[1,1,26214...) fusion(f32[1,4,262144]{2,1,0:T(4,128)} %param.3), kind=kLoop, calls=%fused_computation.304 | loop fusion | flops 2359296 | bytes 11534336 | tf_op jit(solution)/shard_map/slice | solution.py:118
  24.9 6.7 %fusion.266 = (f32[1,4,258048]{2,1,0:T(4,128)}, f32[1,4,258048]{2,1,0:T(4,128)}) fusion(f32[1,4,262144]{2,1,0:T(4,128)} %param.3), kind=kLoop, calls=%fused_computation.314 | loop fusion | bytes 16515072 | tf_op jit(solution)/shard_map/jit(_roll_static)/slice | solution.py:23
  36.2 4.5 fusion.263
  40.7 4.5 fusion.260
  56.9 113.4 %all-reduce.2.cloned.1.call-done = f32[3,262144]{1,0:T(4,128)} async-done(((f32[3,262144]{1,0:T(4,128)}), f32[3,262144]{1,0:T(4,128)}) %all-reduce.2.cloned.1.call-update) | async-done | bytes 3145744 | tf_op jit(solution)/shard_map/psum | solution.py:128
  170.3 20.7 %fusion.257 = (f32[1,262144]{1,0:T(1,128)}, f32[262144]{0:T(1024)}, f32[1,262144]{1,0:T(1,128)}, f32[1,262144]{1,0:T(1,128)}) fusion(f32[3,262144]{1,0:T(4,128)} %all-reduce.2.cloned.1.call-done), kind=kLoop, calls=%fused_computation.305 | loop fusion | bytes 7340032 | tf_op jit(solution)/shard_map/slice | solution.py:142
  200.5 4.9 fusion.36
  207.7 4.8 subtract_bitcast_fusion
  216.6 5.0 fusion.92
  221.6 4.9 add_bitcast_fusion
  278.0 28.9 %fusion.6 = f32[1,4,262144]{2,1,0:T(4,128)} fusion(f32[1,4,258048]{2,1,0:T(4,128)} %get-tuple-element.123, f32[1,4,4096]{2,1,0:T(4,128)S(1)} %get-tuple-element.125, f32[1,4,4096]{2,1,0:T(4,128)S(1)} %get-tuple-element.124, f32[1,4,258048]{2,1,0:T(4,128)} %get-tuple-element.122, f32[1,4,258112]{2,1,0:T(4,128)} %get-tuple-element.119, ...), kind=kLoop, calls=%fused_computation.7 | loop fusion | flops 25165824 | bytes 52428800 | tf_op jit(solution)/shard_map/add | solution.py:41
  307.0 10.5 %fusion.255 = (f32[1,1,262144]{2,1,0:T(1,128)S(1)}, f32[1,1,262144]{2,1,0:T(1,128)S(1)}, f32[1,1,262144]{2,1,0:T(1,128)S(1)}, f32[1,1,262144]{2,1,0:T(1,128)S(1)}) fusion(f32[1,4,262144]{2,1,0:T(4,128)} %fusion.6), kind=kLoop, calls=%fused_computation.303 | loop fusion | bytes 8388608 | tf_op jit(solution)/shard_map/slice | solution.py:42
  332.5 4.5 fusion.250
  337.0 4.8 fusion.247
  347.0 41.1 %fusion.13 = f32[1,4,262144]{2,1,0:T(4,128)} fusion(f32[1,4,258048]{2,1,0:T(4,128)} %get-tuple-element.86, f32[1,4,4096]{2,1,0:T(4,128)S(1)} %get-tuple-element.88, f32[1,4,4096]{2,1,0:T(4,128)S(1)} %get-tuple-element.87, f32[1,4,258048]{2,1,0:T(4,128)} %get-tuple-element.85, f32[1,4,258112]{2,1,0:T(4,128)} %get-tuple-element.82, ...), kind=kLoop, calls=%fused_computation.21 | loop fusion | flops 28311552 | bytes 52428800 | tf_op jit(solution)/shard_map/add | solution.py:41
  388.2 10.5 %fusion.244 = (f32[1,1,262144]{2,1,0:T(1,128)S(1)}, f32[1,1,262144]{2,1,0:T(1,128)S(1)}, f32[1,1,262144]{2,1,0:T(1,128)S(1)}, f32[1,1,262144]{2,1,0:T(1,128)S(1)}) fusion(f32[1,4,262144]{2,1,0:T(4,128)} %fusion.13), kind=kLoop, calls=%fused_computation.292 | loop fusion | bytes 8388608 | tf_op jit(solution)/shard_map/slice | solution.py:43
  408.4 4.6 fusion.240
  413.8 4.5 fusion.239
  427.8 41.1 %fusion.20 = f32[1,4,262144]{2,1,0:T(4,128)} fusion(f32[1,4,258048]{2,1,0:T(4,128)} %get-tuple-element.58, f32[1,4,4096]{2,1,0:T(4,128)S(1)} %get-tuple-element.60, f32[1,4,4096]{2,1,0:T(4,128)S(1)} %get-tuple-element.59, f32[1,4,258048]{2,1,0:T(4,128)} %get-tuple-element.57, f32[1,4,258112]{2,1,0:T(4,128)} %get-tuple-element.54, ...), kind=kLoop, calls=%fused_computation.34 | loop fusion | flops 28311552 | bytes 52428800 | tf_op jit(solution)/shard_map/add | solution.py:41
  469.0 10.5 %fusion.233 = (f32[1,1,262144]{2,1,0:T(1,128)S(1)}, f32[1,1,262144]{2,1,0:T(1,128)S(1)}, f32[1,1,262144]{2,1,0:T(1,128)S(1)}, f32[1,1,262144]{2,1,0:T(1,128)S(1)}) fusion(f32[1,4,262144]{2,1,0:T(4,128)} %fusion.20), kind=kLoop, calls=%fused_computation.281 | loop fusion | bytes 8388608 | tf_op jit(solution)/shard_map/slice | solution.py:43
  495.8 4.5 fusion.228
  514.6 41.1 %fusion.27 = f32[1,4,262144]{2,1,0:T(4,128)} fusion(f32[1,4,258048]{2,1,0:T(4,128)} %get-tuple-element.34, f32[1,4,4096]{2,1,0:T(4,128)S(1)} %get-tuple-element.36, f32[1,4,4096]{2,1,0:T(4,128)S(1)} %get-tuple-element.35, f32[1,4,258048]{2,1,0:T(4,128)} %get-tuple-element.33, f32[1,4,258112]{2,1,0:T(4,128)} %get-tuple-element.30, ...), kind=kLoop, calls=%fused_computation.47 | loop fusion | flops 28311552 | bytes 52428800 | tf_op jit(solution)/shard_map/add | solution.py:41
  555.7 11.5 %fusion.222 = (f32[1,1,262144]{2,1,0:T(1,128)S(1)}, f32[1,1,262144]{2,1,0:T(1,128)S(1)}, f32[1,1,262144]{2,1,0:T(1,128)S(1)}, f32[1,1,262144]{2,1,0:T(1,128)}) fusion(f32[1,4,262144]{2,1,0:T(4,128)} %fusion.27), kind=kLoop, calls=%fused_computation.270 | loop fusion | bytes 8388608 | tf_op jit(solution)/shard_map/slice | solution.py:43
  571.9 16.1 %maximum_add_fusion.4 = f32[1,4,262144]{2,1,0:T(4,128)} fusion(f32[1,1,262144]{2,1,0:T(1,128)S(1)} %bitcast.185, f32[1,1,262144]{2,1,0:T(1,128)S(1)} %bitcast.186, f32[1,1,262144]{2,1,0:T(1,128)S(1)} %bitcast.184, f32[1,1,262144]{2,1,0:T(1,128)S(1)} %bitcast.183, f32[1,4,262144]{2,1,0:T(4,128)S(1)} %copy-done.2, f32[1,1,262144]{2,1,0:T(1,128)S(1)} %bitcast.155, ...), kind=kLoop, calls=%fused_computation.52 | loop fusion | flops 16777216 | bytes 25165824 | tf_op jit(solution)/shard_map/add | solution.py:65
  (196 shorter events, 163.6 us)
Async XLA Ops:
  7.2 163.2 %all-reduce.2.cloned.1.call-start = ((), (), s32[]{:S(2)}) async-start(), calls=%async_computation | async-start | bytes 8388608 | tf_op jit(solution)/shard_map/psum | solution.py:128
  53.4 224.7 %copy-start.49 = (pred[262144]{0:T(1024)(128)(4,1)}, pred[262144]{0:T(1024)(128)(4,1)S(1)}, u32[]{:S(2)}) copy-start(pred[262144]{0:T(1024)(128)(4,1)S(1)} %get-tuple-element.134) | copy-start | bytes 786436
  54.3 223.7 %copy-start.50 = (pred[262144]{0:T(1024)(128)(4,1)}, pred[262144]{0:T(1024)(128)(4,1)S(1)}, u32[]{:S(2)}) copy-start(pred[262144]{0:T(1024)(128)(4,1)S(1)} %get-tuple-element.135) | copy-start | bytes 786436
  306.9 10.6 %copy-start.39 = (f32[1,1,262144]{2,1,0:T(1,128)S(1)}, f32[1,1,262144]{2,1,0:T(1,128)}, u32[]{:S(2)}) copy-start(f32[1,1,262144]{2,1,0:T(1,128)} %get-tuple-element.99) | copy-start | bytes 3145732
  306.9 10.6 %copy-start.40 = (f32[1,1,262144]{2,1,0:T(1,128)S(1)}, f32[1,1,262144]{2,1,0:T(1,128)}, u32[]{:S(2)}) copy-start(f32[1,1,262144]{2,1,0:T(1,128)} %get-tuple-element.100) | copy-start | bytes 3145732
  306.9 10.6 %copy-start.51 = (f32[1,262144]{1,0:T(1,128)S(1)}, f32[1,262144]{1,0:T(1,128)}, u32[]{:S(2)}) copy-start(f32[1,262144]{1,0:T(1,128)} %get-tuple-element.102) | copy-start | bytes 3145732
  307.0 10.6 %copy-start.52 = (f32[1,262144]{1,0:T(1,128)S(1)}, f32[1,262144]{1,0:T(1,128)}, u32[]{:S(2)}) copy-start(f32[1,262144]{1,0:T(1,128)} %get-tuple-element.104) | copy-start | bytes 3145732
  388.1 10.6 %copy-start.4 = (f32[262144]{0:T(1024)S(1)}, f32[262144]{0:T(1024)}, u32[]{:S(2)}) copy-start(f32[262144]{0:T(1024)} %copy-done.3) | copy-start | bytes 3145732
  388.2 10.6 %copy-start.8 = (f32[262144]{0:T(1024)S(1)}, f32[262144]{0:T(1024)}, u32[]{:S(2)}) copy-start(f32[262144]{0:T(1024)} %copy-done.7) | copy-start | bytes 3145732
  388.2 10.6 %copy-start.12 = (f32[262144]{0:T(1024)S(1)}, f32[262144]{0:T(1024)}, u32[]{:S(2)}) copy-start(f32[262144]{0:T(1024)} %copy-done.11) | copy-start | bytes 3145732
  468.9 10.6 %copy-start.5 = (f32[262144]{0:T(1024)S(1)}, f32[262144]{0:T(1024)}, u32[]{:S(2)}) copy-start(f32[262144]{0:T(1024)} %copy-done.3) | copy-start | bytes 3145732
  468.9 10.6 %copy-start.9 = (f32[262144]{0:T(1024)S(1)}, f32[262144]{0:T(1024)}, u32[]{:S(2)}) copy-start(f32[262144]{0:T(1024)} %copy-done.7) | copy-start | bytes 3145732
  468.9 10.6 %copy-start.13 = (f32[262144]{0:T(1024)S(1)}, f32[262144]{0:T(1024)}, u32[]{:S(2)}) copy-start(f32[262144]{0:T(1024)} %copy-done.11) | copy-start | bytes 3145732
  468.9 10.6 %copy-start.32 = (f32[1,1,262144]{2,1,0:T(1,128)S(1)}, f32[1,1,262144]{2,1,0:T(1,128)}, u32[]{:S(2)}) copy-start(f32[1,1,262144]{2,1,0:T(1,128)} %copy-done.31) | copy-start | bytes 3145732
  468.9 10.6 %copy-start.34 = (f32[1,1,262144]{2,1,0:T(1,128)S(1)}, f32[1,1,262144]{2,1,0:T(1,128)}, u32[]{:S(2)}) copy-start(f32[1,1,262144]{2,1,0:T(1,128)} %copy-done.33) | copy-start | bytes 3145732
  469.0 10.6 %copy-start.36 = (f32[1,1,262144]{2,1,0:T(1,128)S(1)}, f32[1,1,262144]{2,1,0:T(1,128)}, u32[]{:S(2)}) copy-start(f32[1,1,262144]{2,1,0:T(1,128)} %copy-done.35) | copy-start | bytes 3145732
  469.0 10.6 %copy-start.38 = (f32[1,1,262144]{2,1,0:T(1,128)S(1)}, f32[1,1,262144]{2,1,0:T(1,128)}, u32[]{:S(2)}) copy-start(f32[1,1,262144]{2,1,0:T(1,128)} %copy-done.37) | copy-start | bytes 3145732
  555.7 11.6 %copy-start.16 = (f32[262144]{0:T(1024)S(1)}, f32[262144]{0:T(1024)}, u32[]{:S(2)}) copy-start(f32[262144]{0:T(1024)} %copy-done.15) | copy-start | bytes 3145732
  555.7 11.6 %copy-start.18 = (f32[262144]{0:T(1024)S(1)}, f32[262144]{0:T(1024)}, u32[]{:S(2)}) copy-start(f32[262144]{0:T(1024)} %copy-done.17) | copy-start | bytes 3145732
  555.7 11.6 %copy-start.20 = (f32[262144]{0:T(1024)S(1)}, f32[262144]{0:T(1024)}, u32[]{:S(2)}) copy-start(f32[262144]{0:T(1024)} %copy-done.19) | copy-start | bytes 3145732
  555.7 11.6 %copy-start.22 = (f32[262144]{0:T(1024)S(1)}, f32[262144]{0:T(1024)}, u32[]{:S(2)}) copy-start(f32[262144]{0:T(1024)} %copy-done.21) | copy-start | bytes 3145732
  571.9 16.1 %copy-start.53 = (f32[1,64,4096]{2,1,0:T(8,128)S(1)}, f32[1,64,4096]{2,1,0:T(8,128)}, u32[]{:S(2)}) copy-start(f32[1,64,4096]{2,1,0:T(8,128)} %stack.101) | copy-start | bytes 3145732
  571.9 16.1 %copy-start.54 = (f32[1,64,4096]{2,1,0:T(8,128)S(1)}, f32[1,64,4096]{2,1,0:T(8,128)}, u32[]{:S(2)}) copy-start(f32[1,64,4096]{2,1,0:T(8,128)} %stack.100) | copy-start | bytes 3145732
  571.9 16.1 %copy-start.55 = (f32[1,64,4096]{2,1,0:T(8,128)S(1)}, f32[1,64,4096]{2,1,0:T(8,128)}, u32[]{:S(2)}) copy-start(f32[1,64,4096]{2,1,0:T(8,128)} %stack.99) | copy-start | bytes 3145732
  (37 other events, 141.4 us)
Sparse Core Ops, SparseCore 0:
  25.1 145.2 all-reduce.1
where the time goes:
time: 604 us; the launch traced here: 596 us
  other arithmetic  209 us (35%)
  local copies, waits for them, and re-layouts  190 us (31%)
  waiting for transfers between devices  113 us (19%)
  matrix products  68.9 us (11%)
  between operations  15.4 us (3%)
    add x4, other arithmetic, hamiltonian(): single = -kinetic_coef * laplace + mean_field * state  152 us
    psum x1, waiting for transfers between devices, local(): summed = lax.psum(partial_value, ('grp', 'wf'))  113 us
    dot_general x22, matrix products, apply(): return jnp.dot(values, matrix, precision=lax.Precision.HIGHEST)  68.9 us
    slice x3, local copies, waits for them, and re-layouts, hamiltonian(): single[..., 1, :] + pair_real * state[..., 3, :]  32.6 us
    slice x8, local copies, waits for them, and re-layouts, neighbour_sum(): jnp.roll(field, -(grid - 1) * grid, -1)  21.8 us
    slice x1, local copies, waits for them, and re-layouts, local(): summed[2]  20.7 us
    slice x8, local copies, waits for them, and re-layouts, neighbour_sum(): jnp.roll(field, 1, -1)  19.6 us
    slice x8, local copies, waits for them, and re-layouts, neighbour_sum(): jnp.roll(field, 1 - grid, -1)  18.5 us
  transfers between devices with their start and end apart: 1, of which 1 were waited for; matrix products, arithmetic and copies ran while one was open for 5% of the time, Pallas kernels for 0%

commit v1 on v0

v1 whole, which is shorter than its diff:
```python
import functools
import math

import jax
import jax.numpy as jnp
import numpy as np
from jax import lax
from jax.experimental import pallas as pl
from jax.experimental.pallas import tpu as pltpu
from jax.sharding import PartitionSpec as P

NX = 64
NG = 64
LANES = 2 * NG
PLANE = NG * NG // LANES
ROWS = NX * PLANE
AXES = ("grp", "wf")
GROUP = 4
PAD = 8
PADDED = PLANE + 2 * PAD

time_step = 0.2
kinetic_coef = 0.5
density_coef = 1.0
coulomb_coef = 0.25

F32 = jnp.float32
BF16 = jnp.bfloat16


def fourier_basis(length):
    cells = np.arange(length)
    rows, waves = [np.ones(length) / math.sqrt(length)], [0]
    for wave in range(1, length // 2):
        angle = 2.0 * math.pi * (wave * cells % length) / length
        rows += [math.sqrt(2.0 / length) * np.cos(angle), math.sqrt(2.0 / length) * np.sin(angle)]
        waves += [wave, wave]
    rows.append(np.where(cells % 2 == 0, 1.0, -1.0) / math.sqrt(length))
    waves.append(length // 2)
    return np.stack(rows), np.array(waves)


def lattice_symbol(waves, length):
    return 2.0 - 2.0 * np.cos(2.0 * math.pi / length * waves)


def split(matrix):
    high = matrix.astype(np.float32).astype(jnp.bfloat16)
    low = (matrix - high.astype(np.float64)).astype(jnp.bfloat16)
    return np.stack([high, low])


def block_diagonal(matrix, count):
    return np.kron(np.eye(count), matrix)


def transform_tables():
    basis, waves = fourier_basis(NG)
    order = np.concatenate([np.arange(0, NG, 2), np.arange(1, NG, 2)])
    forward_y = block_diagonal(basis[:, order], GROUP)
    forward_z = block_diagonal(basis.T, 2)
    first, first_waves = fourier_basis(NX)
    even, odd = first_waves % 2 == 0, first_waves % 2 == 1
    symbol_x = lattice_symbol(first_waves, NX)
    symbol = lattice_symbol(waves, NG)
    symbol_xz = np.concatenate(
        [symbol_x[even][:, None] + symbol[None], symbol_x[odd][:, None] + symbol[None]], axis=1
    )
    return dict(
        forward_y=split(forward_y),
        forward_z=split(forward_z),
        inverse_y=split(forward_y.T),
        inverse_z=split(forward_z.T),
        even=first[even][:, : NX // 2].astype(np.float32),
        odd=first[odd][:, : NX // 2].astype(np.float32),
        symbol_xz=symbol_xz.astype(np.float32),
        symbol_y=symbol.astype(np.float32),
    )


class Plan:
    def __init__(self, sizes, orders, pieces):
        self.sizes = sizes
        self.orders = orders
        self.pieces = pieces
        self.halvings = int(math.log2(pieces)) - 1
        kept = [("grp", 1)] + sorted(orders[0][: self.halvings])
        assert kept[1:] == sorted(orders[1][: self.halvings])
        self.kept = kept

    def permutation(self, step):
        pairs = []
        for grp in range(self.sizes["grp"]):
            for wf in range(self.sizes["wf"]):
                axis, mask = ("grp", 1) if step < 0 else self.orders[grp & 1][step]
                to = (grp ^ mask, wf) if axis == "grp" else (grp, wf ^ mask)
                pairs.append((grp * self.sizes["wf"] + wf, to[0] * self.sizes["wf"] + to[1]))
        return pairs

    def identity(self, grp, wf):
        number = 0
        for place, (axis, mask) in enumerate(self.kept):
            value = grp if axis == "grp" else wf
            number = number + (((value >> int(math.log2(mask))) & 1) << place)
        return number

    def piece(self, index, side):
        grp, wf = lax.axis_index("grp"), lax.axis_index("wf")
        core = (grp & 1) ^ side
        grp = grp ^ side
        for step in range(self.halvings):
            bit = (index >> (self.halvings - 1 - step)) & 1
            masks = [
                [mask if axis == name else 0 for axis, mask in (self.orders[0][step], self.orders[1][step])]
                for name in AXES
            ]
            grp_mask = masks[0][0] + core * (masks[0][1] - masks[0][0])
            wf_mask = masks[1][0] + core * (masks[1][1] - masks[1][0])
            grp = grp ^ (bit * grp_mask)
            wf = wf ^ (bit * wf_mask)
        return self.identity(grp, wf)


def reduce_scatter(plan, own, other):
    for step in range(-1, len(plan.orders[0])):
        received = lax.ppermute(other, AXES, plan.permutation(step))
        if step + 1 == len(plan.orders[0]):
            break
        if step + 1 < plan.halvings:
            half = own.shape[0] // 2
            own, other = own[:half] + received[:half], own[half:] + received[half:]
        else:
            own = own + received
            other = own
    return own, received


def all_gather(plan, piece):
    parts = [piece]
    for step in reversed(range(plan.halvings)):
        whole = parts[0] if len(parts) == 1 else jnp.concatenate(parts)
        parts = [whole, lax.ppermute(whole, AXES, plan.permutation(step))]
    return parts + [lax.ppermute(part, AXES, plan.permutation(-1)) for part in parts]


def lane(shape):
    return lax.broadcasted_iota(jnp.int32, shape, len(shape) - 1)


def swap(value):
    return pltpu.roll(value, NG, value.ndim - 1)


def cut(value):
    high = value.astype(BF16)
    return high, (value - high.astype(F32)).astype(BF16)


def product(left, right):
    return lax.dot_general(left, right, (((1,), (0,)), ((), ())), preferred_element_type=F32)


def times_table(value, table):
    high, low = cut(value)
    return product(high, table[0]) + (product(low, table[0]) + product(high, table[1]))


def table_times(table, value):
    high, low = cut(value)
    return product(table[0], high) + (product(table[0], low) + product(table[1], high))


def component(state_ref, wave, index, row, rows):
    return state_ref[pl.ds((wave * ROWS + row) * 4 + index, rows, stride=4), :]


def kappa_kernel(plans, waves, scale, state_ref, *out_refs):
    for which, plan in enumerate(plans):
        rows = ROWS // plan.pieces
        for side in range(2):
            out_ref = out_refs[2 * which + side]

            def body(index, carry, plan=plan, side=side, out_ref=out_ref, which=which, rows=rows):
                row = plan.piece(index, side) * rows
                total = None
                for wave in range(waves):
                    u_real, u_imag, v_real, v_imag = (
                        component(state_ref, wave, c, row, rows) for c in range(4)
                    )
                    if which == 0:
                        value = u_real * v_real + u_imag * v_imag
                    else:
                        value = u_imag * v_real - u_real * v_imag
                    total = value if total is None else total + value
                out_ref[index] = total * scale
                return carry

            lax.fori_loop(0, plan.pieces // 2, body, 0)


def density_kernel(plan, waves, scale, state_ref, y_ref, z_ref, own_ref, other_ref, spectrum_ref):
    low_lanes = lane((PLANE, LANES)) < NG
    half = NX // 2

    def density(plane):
        total = None
        for wave in range(waves):
            real = component(state_ref, wave, 2, plane * PLANE, PLANE)
            imag = component(state_ref, wave, 3, plane * PLANE, PLANE)
            value = real * real + imag * imag
            total = value if total is None else total + value
        return total * scale

    def body(group, carry):
        parts = []
        for j in range(GROUP):
            plane = group * GROUP + j
            first, second = density(plane), density(plane + half)
            parts.append(jnp.where(low_lanes, first, swap(second)))
            parts.append(jnp.where(low_lanes, swap(first), second))
        value = times_table(jnp.concatenate(parts), z_ref)
        value = table_times(y_ref, value)
        for j in range(GROUP):
            spectrum_ref[pl.ds(group * GROUP + j, NG, stride=half), :] = value[j * NG : (j + 1) * NG]
        return carry

    lax.fori_loop(0, half // GROUP, body, 0)
    rows = ROWS // plan.pieces
    for side, out_ref in enumerate((own_ref, other_ref)):

        def place(index, carry, side=side, out_ref=out_ref):
            start = pl.multiple_of(plan.piece(index, side) * rows, 8)
            out_ref[index] = spectrum_ref[pl.ds(start, rows), :]
            return carry

        lax.fori_loop(0, plan.pieces // 2, place, 0)


def coulomb_kernel(plan, own_ref, received_ref, even_ref, odd_ref, xz_ref, y_ref, out_ref):
    half = NX // 2
    low_lanes = lane((half, LANES)) < NG
    sign = jnp.where(low_lanes, 1.0, -1.0)
    count = ROWS // plan.pieces // half
    first = plan.identity(lax.axis_index("grp"), lax.axis_index("wf")) * count

    def dot(matrix, value, axis):
        return lax.dot_general(
            matrix, value, (((axis,), (0,)), ((), ())),
            precision=lax.Precision.HIGHEST, preferred_element_type=F32,
        )

    for k in range(count):
        rows = pl.ds(k * half, half)
        value = own_ref[0, rows, :] + received_ref[0, rows, :]
        value = swap(value) + sign * value
        value = jnp.where(low_lanes, dot(even_ref[...], value, 1), dot(odd_ref[...], value, 1))
        squared = xz_ref[...] + y_ref[first + k]
        kernel = jnp.where(
            squared > 0.001,
            4.0 * math.pi * coulomb_coef / jnp.where(squared > 0.001, squared, 1.0),
            0.0,
        )
        value = value * (density_coef + kernel)
        value = jnp.where(low_lanes, dot(even_ref[...], value, 0), dot(odd_ref[...], value, 0))
        out_ref[0, rows, :] = swap(value) + sign * value


def spread(plan, part_refs, store):
    count = plan.pieces // 4
    for side in range(2):
        for part in range(2):
            ref = part_refs[2 * side + part]

            def body(index, carry, side=side, part=part, ref=ref):
                store(plan.piece(index + part * count, side), ref[index])
                return carry

            lax.fori_loop(0, count, body, 0)


def mean_kernel(plan, *refs):
    part_refs, (outer_ref, y_ref, z_ref, out_ref, spectrum_ref) = refs[:4], refs[4:]
    rows = ROWS // plan.pieces
    half = NX // 2
    low_lanes = lane((PLANE, LANES)) < NG

    def store(piece, value):
        spectrum_ref[pl.ds(pl.multiple_of(piece * rows, 8), rows), :] = value

    spread(plan, part_refs, store)

    def body(group, carry):
        value = jnp.concatenate(
            [spectrum_ref[pl.ds(group * GROUP + j, NG, stride=half), :] for j in range(GROUP)]
        )
        value = table_times(y_ref, value)
        value = times_table(value, z_ref)
        for j in range(GROUP):
            plane = group * GROUP + j
            even = value[j * NG : j * NG + PLANE]
            odd = value[j * NG + PLANE : (j + 1) * NG]
            near = pl.ds(pl.multiple_of(plane * PLANE, 8), PLANE)
            far = pl.ds(pl.multiple_of((plane + half) * PLANE, 8), PLANE)
            out_ref[near, :] = jnp.where(low_lanes, even, swap(odd)) + outer_ref[near, :]
            out_ref[far, :] = jnp.where(low_lanes, swap(even), odd) + outer_ref[far, :]
        return carry

    lax.fori_loop(0, half // GROUP, body, 0)


def propagate_kernel(plans, *refs):
    (state_ref, mean_ref, coupling_ref), refs = refs[:3], refs[3:]
    parts, refs = (refs[:4], refs[4:8]), refs[8:]
    out_ref, potentials_ref, shifted_ref, pair_real_ref, pair_imag_ref, psi_ref, ping_ref, pong_ref = refs
    pairs = (pair_real_ref, pair_imag_ref)

    for plan, part_refs, pair_ref in zip(plans, parts, pairs):
        rows = ROWS // plan.pieces

        def store(piece, value, pair_ref=pair_ref, rows=rows):
            where = pl.ds(pl.multiple_of(piece * rows, 8), rows)
            pair_ref[where, :] = -coupling_ref[where, :] * value

        spread(plan, part_refs, store)

    planes, width = potentials_ref.shape[1:]
    start = lax.axis_index("grp") * planes * PLANE + lax.axis_index("wf") * (width // LANES)
    for which, ref in enumerate((mean_ref, pair_real_ref, pair_imag_ref)):
        for j in range(width // LANES):
            potentials_ref[which, :, j * LANES : (j + 1) * LANES] = ref[pl.ds(start + j, planes, stride=PLANE), :]

    def write(ref, c, plane, chunk, value):
        base = pl.multiple_of(plane * PADDED, 8)
        ref[c, pl.ds(base + PAD + chunk * 8, 8), :] = value
        if chunk == 0:
            ref[c, pl.ds(base + PAD + PLANE, 1), :] = value[:1]
        if chunk == PLANE // 8 - 1:
            ref[c, pl.ds(base + PAD - 1, 1), :] = value[7:]

    def prepare(plane, carry):
        for chunk in range(PLANE // 8):
            row = plane * PLANE + chunk * 8
            where = pl.ds(pl.multiple_of(row, 8), 8)
            shifted_ref[where, :] = mean_ref[where, :] + 6.0 * kinetic_coef
            for c in range(4):
                write(psi_ref, c, plane, chunk, component(state_ref, 0, c, row, 8))
        return carry

    lax.fori_loop(0, NX, prepare, 0)

    lanes = lane((8, LANES))
    high_lanes = lanes >= NG
    last_depth = lanes % NG == NG - 1
    first_depth = lanes % NG == 0

    def stage(degree, source, target):
        factor = time_step / degree

        def body(plane, carry):
            base = pl.multiple_of(plane * PADDED, 8)
            before = pl.multiple_of((plane + NX - 1) % NX * PADDED, 8)
            after = pl.multiple_of((plane + 1) % NX * PADDED, 8)
            for chunk in range(PLANE // 8):
                offset = PAD + chunk * 8
                row = plane * PLANE + chunk * 8
                where = pl.ds(pl.multiple_of(row, 8), 8)
                shifted, pair_real, pair_imag = shifted_ref[where, :], pair_real_ref[where, :], pair_imag_ref[where, :]
                state, single = [], []
                for c in range(4):
                    here = source[c, pl.ds(base + offset, 8), :]
                    total = source[c, pl.ds(before + offset, 8), :] + source[c, pl.ds(after + offset, 8), :]
                    other = swap(here)
                    side = jnp.where(
                        high_lanes,
                        source[c, pl.ds(base + offset - 1, 8), :],
                        source[c, pl.ds(base + offset + 1, 8), :],
                    )
                    total = total + other + swap(side)
                    total = total + pltpu.roll(jnp.where(last_depth, other, here), 1, 1)
                    total = total + pltpu.roll(jnp.where(first_depth, other, here), LANES - 1, 1)
                    state.append(here)
                    single.append(shifted * here - kinetic_coef * total)
                applied = (
                    single[0] + pair_real * state[2] - pair_imag * state[3],
                    single[1] + pair_real * state[3] + pair_imag * state[2],
                    pair_real * state[0] + pair_imag * state[1] - single[2],
                    pair_real * state[1] - pair_imag * state[0] - single[3],
                )
                turned = (factor * applied[1], -factor * applied[0], factor * applied[3], -factor * applied[2])
                for c in range(4):
                    psi = state[c] if source is psi_ref else psi_ref[c, pl.ds(base + offset, 8), :]
                    value = psi + turned[c]
                    if target is None:
                        out_ref[pl.ds(row * 4 + c, 8, stride=4), :] = value
                    else:
                        write(target, c, plane, chunk, value)
            return carry

        lax.fori_loop(0, NX, body, 0)

    stage(4, psi_ref, ping_ref)
    stage(3, ping_ref, pong_ref)
    stage(2, pong_ref, ping_ref)
    stage(1, ping_ref, None)


def vmem(count):
    return [pl.BlockSpec(memory_space=pltpu.VMEM)] * count


def call(kernel, name, out_shapes, operands, scratch=(), in_specs=None, flops=0):
    moved = sum(math.prod(o.shape) * 4 for o in out_shapes) + sum(math.prod(o.shape) * 4 for o in operands)
    return pl.pallas_call(
        kernel,
        name=name,
        out_shape=[jax.ShapeDtypeStruct(o.shape, o.dtype) for o in out_shapes],
        in_specs=in_specs or vmem(len(operands)),
        out_specs=vmem(len(out_shapes)),
        scratch_shapes=[pltpu.VMEM(shape, F32) for shape in scratch],
        compiler_params=pltpu.CompilerParams(vmem_limit_bytes=56 * 1024 * 1024),
        cost_estimate=pl.CostEstimate(flops=flops, bytes_accessed=moved, transcendentals=0),
    )(*operands)


def like(*shape):
    return jax.ShapeDtypeStruct(shape, F32)


def local(quasi, outer_field, coupling):
    sizes = {name: lax.axis_size(name) for name in AXES}
    devices = sizes["grp"] * sizes["wf"]
    waves = quasi.shape[0]
    scale = 1.0 / (waves * devices)
    bits = [("grp", 1 << k) for k in range(1, sizes["grp"].bit_length() - 1)]
    bits += [("wf", 1 << k) for k in range(sizes["wf"].bit_length() - 1)]
    first, second, third, rest = bits[0], bits[1], bits[2], bits[3:]
    straight = [first, second, third] + rest
    crossed = [second, first, third] + rest
    real_plan = Plan(sizes, (straight, crossed), devices)
    imag_plan = Plan(sizes, (crossed, straight), devices)
    mean_plan = Plan(sizes, ([third, first, second] + rest, [third, second, first] + rest), min(devices, NG))
    tables = {name: jnp.asarray(table) for name, table in transform_tables().items()}

    def halves(plan):
        return [like(plan.pieces // 2, ROWS // plan.pieces, LANES)] * 2

    state = quasi.reshape(waves, 4, ROWS, LANES).transpose(0, 2, 1, 3).reshape(waves * ROWS * 4, LANES)
    outer_field = outer_field.reshape(ROWS, LANES)
    coupling = coupling.reshape(ROWS, LANES)

    real_own, real_other, imag_own, imag_other = call(
        functools.partial(kappa_kernel, (real_plan, imag_plan), waves, scale),
        "kappa", halves(real_plan) + halves(imag_plan), [state],
    )
    mean_own, mean_other = call(
        functools.partial(density_kernel, mean_plan, waves, scale),
        "density", halves(mean_plan), [state, tables["forward_y"], tables["forward_z"]], [(ROWS, LANES)],
    )
    real = reduce_scatter(real_plan, real_own, real_other)
    imag = reduce_scatter(imag_plan, imag_own, imag_other)
    mean = reduce_scatter(mean_plan, mean_own, mean_other)
    (spectrum,) = call(
        functools.partial(coulomb_kernel, mean_plan),
        "coulomb", [like(*mean[0].shape)],
        [*mean, tables["even"], tables["odd"], tables["symbol_xz"], tables["symbol_y"]],
        in_specs=vmem(5) + [pl.BlockSpec(memory_space=pltpu.SMEM)],
    )
    mean_parts = all_gather(mean_plan, spectrum)
    real_parts = all_gather(real_plan, real[0] + real[1])
    imag_parts = all_gather(imag_plan, imag[0] + imag[1])
    (mean_field,) = call(
        functools.partial(mean_kernel, mean_plan),
        "mean", [like(ROWS, LANES)],
        [*mean_parts, outer_field, tables["inverse_y"], tables["inverse_z"]], [(ROWS, LANES)],
    )

    padded = (4, NX * PADDED, LANES)
    evolved = []
    for wave in range(waves):
        own_state = state[wave * ROWS * 4 : (wave + 1) * ROWS * 4]
        evolved_rows, potentials = call(
            functools.partial(propagate_kernel, (real_plan, imag_plan)),
            "propagate",
            [like(ROWS * 4, LANES), like(3, NX // sizes["grp"], NG * NG // sizes["wf"])],
            [own_state, mean_field, coupling, *real_parts, *imag_parts],
            [(ROWS, LANES)] * 3 + [padded] * 3,
        )
        evolved.append(evolved_rows)
    evolved = jnp.concatenate(evolved) if waves > 1 else evolved[0]
    evolved = evolved.reshape(waves, ROWS, 4, LANES).transpose(0, 2, 1, 3).reshape(quasi.shape)
    return (evolved, potentials)


def solution(mesh):
    placed = (P(AXES, None, None), P(), P())
    return jax.shard_map(
        local,
        mesh=mesh,
        in_specs=placed,
        out_specs=(P(AXES, None, None), P(None, "grp", "wf")),
        check_vma=False,
    )
```

time: 604 us -> 137 us (0.23); the launches traced: 596 us -> 137 us
  other arithmetic: 209 us -> 5.44 us
  local copies, waits for them, and re-layouts: 190 us -> 2.23 us
  waiting for transfers between devices: 113 us -> 11.5 us
  Pallas kernels: 0 us -> 77.6 us
  matrix products: 68.9 us -> 0 us
  starting transfers between devices: 0.04 us -> 39.2 us
  between operations: 15.4 us -> 0.86 us
    add x7 -> x14, other arithmetic: 172 us -> 3.06 us  [the longest x12 3.04 us: reduce_scatter(): own, other = (own[:half] + received[:half], own[half:] + received[half:])]
    slice x45 -> x0, local copies, waits for them, and re-layouts: 160 us -> none  [the longest x3 32.6 us: hamiltonian(): single[..., 1, :] + pair_real * state[..., 3, :]]
    psum x1 -> x0, waiting for transfers between devices: 113 us -> none  [local(): summed = lax.psum(partial_value, ('grp', 'wf'))]
    pallas_call x0 -> x5, Pallas kernels: none -> 77.6 us  [call(): pl.pallas_call(kernel, name=name, out_shape=[jax.ShapeDtypeStruct(o.shape...]
    dot_general x22 -> x0, matrix products: 68.9 us -> none  [apply(): return jnp.dot(values, matrix, precision=lax.Precision.HIGHEST)]
    ppermute x0 -> x33, starting transfers between devices: none -> 39.2 us  [the longest x15 22.4 us: reduce_scatter(): received = lax.ppermute(other, AXES, plan.permutation(step))]
    slice x1 -> x0, other arithmetic: 13.3 us -> none  [local(): quasi[:, 0] * quasi[:, 2] + quasi[:, 1] * quasi[:, 3]]
    another operation x4 -> x0, other arithmetic: 12.9 us -> none  [the longest x3 12.2 us: propagate(): jnp.stack([factor * applied[..., 1, :], -factor * applied[..., 0, :], fac...]
  transfers between devices with their start and end apart: 1 -> 33, of which waited for: 1 -> 9; matrix products, arithmetic and copies ran while one was open for 5% -> 4% of each run, Pallas kernels for 0% -> 12%
where the time goes in v1:
time: 137 us
  Pallas kernels  77.6 us (57%)
  starting transfers between devices  39.2 us (29%)
  waiting for transfers between devices  11.5 us (8%)
  other arithmetic  5.44 us (4%)
  local copies, waits for them, and re-layouts  2.23 us (2%)
    pallas_call x5, Pallas kernels, call(): pl.pallas_call(kernel, name=name, out_shape=[jax.ShapeDtypeStruct(o.shape...  77.6 us
    ppermute x15, starting transfers between devices, reduce_scatter(): received = lax.ppermute(other, AXES, plan.permutation(step))  22.4 us
    ppermute x12, starting transfers between devices, all_gather(): parts = [whole, lax.ppermute(whole, AXES, plan.permutation(step))]  15.6 us
    ppermute x12, waiting for transfers between devices, all_gather(): parts = [whole, lax.ppermute(whole, AXES, plan.permutation(step))]  8.34 us
    ppermute x15, waiting for transfers between devices, reduce_scatter(): received = lax.ppermute(other, AXES, plan.permutation(step))  3.13 us
    add x12, other arithmetic, reduce_scatter(): own, other = (own[:half] + received[:half], own[half:] + received[half:])  3.04 us
  transfers between devices with their start and end apart: 33, of which 9 were waited for; matrix products, arithmetic and copies ran while one was open for 4% of the time, Pallas kernels for 12%

profile of v1, /device:TPU:0, one launch (start us, length us, event | category | flops | bytes accessed | tf_op | source)
XLA Modules:
  0.0 136.8 jit_solution(5984467254236123928)
XLA Ops:
  0.6 9.0 %density.1 = (f32[16,64,128]{2,1,0:T(8,128)}, f32[16,64,128]{2,1,0:T(8,128)}) custom-call(f32[8192,128]{1,0:T(8,128)} %bitcast.12, bf16[2,256,256]{2,1,0:T(8,128)(2,1)} %constant.16.clone.y_ref, bf16[2,128,128]{2,1,0:T(8,128)(2,1)} %constant.17.clone.z_ref), custom_call_target="tpu_custom_call" | custom-call | bytes 5898240 | tf_op jit(solution)/shard_map/density/pallas_call | solution.py:413
  10.2 5.5 %kappa.1 = (f32[16,64,128]{2,1,0:T(8,128)}, f32[16,64,128]{2,1,0:T(8,128)}, f32[16,64,128]{2,1,0:T(8,128)}, f32[16,64,128]{2,1,0:T(8,128)}) custom-call(f32[8192,128]{1,0:T(8,128)} %bitcast.13), custom_call_target="tpu_custom_call" | custom-call | bytes 6291456 | tf_op jit(solution)/shard_map/kappa/pallas_call | solution.py:413
  16.2 2.7 %collective-permute-start.1 = (f32[8,64,128]{2,1,0:T(8,128)S(1)}, f32[8,64,128]{2,1,0:T(8,128)S(1)}, u32[]{:S(2)}, u32[]{:S(2)}) collective-permute-start(f32[8,64,128]{2,1,0:T(8,128)S(1)} %get-tuple-element.23), channel_id=1, source_target_pairs={{0,2},{1,3},{2,0},{3,1},{4,6},{5,7},{6,4},{7,5},{8,10},{9,11},{10,... | collective-permute-start | bytes 786440 | tf_op jit(solution)/shard_map/ppermute | solution.py:126
  20.0 1.6 %collective-permute-start.12 = (f32[8,64,128]{2,1,0:T(8,128)S(1)}, f32[8,64,128]{2,1,0:T(8,128)S(1)}, u32[]{:S(2)}, u32[]{:S(2)}) collective-permute-start(f32[8,64,128]{2,1,0:T(8,128)S(1)} %get-tuple-element.21), channel_id=1, source_target_pairs={{0,16},{1,17},{2,18},{3,19},{4,20},{5,21},{6,22},{7,23},{8,9},{9,8... | collective-permute-start | bytes 786440 | tf_op jit(solution)/shard_map/ppermute | solution.py:126
  22.7 1.6 %collective-permute-start.23 = (f32[8,64,128]{2,1,0:T(8,128)S(1)}, f32[8,64,128]{2,1,0:T(8,128)S(1)}, u32[]{:S(2)}, u32[]{:S(2)}) collective-permute-start(f32[8,64,128]{2,1,0:T(8,128)S(1)} %get-tuple-element.19), channel_id=1, source_target_pairs={{0,1},{1,0},{2,3},{3,2},{4,5},{5,4},{6,7},{7,6},{8,24},{9,25},{10,... | collective-permute-start | bytes 786440 | tf_op jit(solution)/shard_map/ppermute | solution.py:126
  24.3 1.6 %collective-permute-done.1 = f32[8,64,128]{2,1,0:T(8,128)S(1)} collective-permute-done((f32[8,64,128]{2,1,0:T(8,128)S(1)}, f32[8,64,128]{2,1,0:T(8,128)S(1)}, u32[]{:S(2)}, u32[]{:S(2)}) %collective-permute-start.1) | collective-permute-done | bytes 262176 | tf_op jit(solution)/shard_map/ppermute | solution.py:126
  25.9 1.7 %collective-permute-start.2 = (f32[4,64,128]{2,1,0:T(8,128)S(1)}, f32[4,64,128]{2,1,0:T(8,128)S(1)}, u32[]{:S(2)}, u32[]{:S(2)}) collective-permute-start(f32[4,64,128]{2,1,0:T(8,128)S(1)} %get-tuple-element.29), channel_id=1, source_target_pairs={{0,16},{1,17},{2,18},{3,19},{4,20},{5,21},{6,22},{7,23},{8,9},{9,8... | collective-permute-start | bytes 393224 | tf_op jit(solution)/shard_map/ppermute | solution.py:126
  27.6 2.7 %collective-permute-start.13 = (f32[4,64,128]{2,1,0:T(8,128)S(1)}, f32[4,64,128]{2,1,0:T(8,128)S(1)}, u32[]{:S(2)}, u32[]{:S(2)}) collective-permute-start(f32[4,64,128]{2,1,0:T(8,128)S(1)} %get-tuple-element.27), channel_id=1, source_target_pairs={{0,1},{1,0},{2,3},{3,2},{4,5},{5,4},{6,7},{7,6},{8,24},{9,25},{10,... | collective-permute-start | bytes 393224 | tf_op jit(solution)/shard_map/ppermute | solution.py:126
  30.3 1.4 %collective-permute-start.24 = (f32[4,64,128]{2,1,0:T(8,128)S(1)}, f32[4,64,128]{2,1,0:T(8,128)S(1)}, u32[]{:S(2)}, u32[]{:S(2)}) collective-permute-start(f32[4,64,128]{2,1,0:T(8,128)S(1)} %get-tuple-element.25), channel_id=1, source_target_pairs={{0,16},{1,17},{2,18},{3,19},{4,20},{5,21},{6,22},{7,23},{8,9},{9,8... | collective-permute-start | bytes 393224 | tf_op jit(solution)/shard_map/ppermute | solution.py:126
  32.2 1.5 %collective-permute-start.3 = (f32[2,64,128]{2,1,0:T(8,128)S(1)}, f32[2,64,128]{2,1,0:T(8,128)S(1)}, u32[]{:S(2)}, u32[]{:S(2)}) collective-permute-start(f32[2,64,128]{2,1,0:T(8,128)S(1)} %get-tuple-element.35), channel_id=1, source_target_pairs={{0,1},{1,0},{2,3},{3,2},{4,5},{5,4},{6,7},{7,6},{8,24},{9,25},{10,... | collective-permute-start | bytes 196616 | tf_op jit(solution)/shard_map/ppermute | solution.py:126
  35.6 1.5 %collective-permute-start.25 = (f32[2,64,128]{2,1,0:T(8,128)S(1)}, f32[2,64,128]{2,1,0:T(8,128)S(1)}, u32[]{:S(2)}, u32[]{:S(2)}) collective-permute-start(f32[2,64,128]{2,1,0:T(8,128)S(1)} %get-tuple-element.31), channel_id=1, source_target_pairs={{0,2},{1,3},{2,0},{3,1},{4,6},{5,7},{6,4},{7,5},{8,10},{9,11},{10,... | collective-permute-start | bytes 196616 | tf_op jit(solution)/shard_map/ppermute | solution.py:126
  37.8 2.6 %collective-permute-start.4 = (f32[1,64,128]{2,1,0:T(8,128)S(1)}, f32[1,64,128]{2,1,0:T(8,128)S(1)}, u32[]{:S(2)}, u32[]{:S(2)}) collective-permute-start(f32[1,64,128]{2,1,0:T(8,128)S(1)} %get-tuple-element.36), channel_id=1, source_target_pairs={{0,4},{1,5},{2,6},{3,7},{4,0},{5,1},{6,2},{7,3},{8,12},{9,13},{10,... | collective-permute-start | bytes 98312 | tf_op jit(solution)/shard_map/ppermute | solution.py:126
  41.6 1.8 %collective-permute-start.26 = (f32[1,64,128]{2,1,0:T(8,128)S(1)}, f32[1,64,128]{2,1,0:T(8,128)S(1)}, u32[]{:S(2)}, u32[]{:S(2)}) collective-permute-start(f32[1,64,128]{2,1,0:T(8,128)S(1)} %slice_add_fusion.18), channel_id=1, source_target_pairs={{0,4},{1,5},{2,6},{3,7},{4,0},{5,1},{6,2},{7,3},{8,12},{9,13},{10,... | collective-permute-start | bytes 98312 | tf_op jit(solution)/shard_map/ppermute | solution.py:126
  44.4 2.1 %coulomb.1 = f32[1,64,128]{2,1,0:T(8,128)} custom-call(f32[1,64,128]{2,1,0:T(8,128)} %get-tuple-element.37.own_ref, f32[1,64,128]{2,1,0:T(8,128)} %copy-done.13, f32[32,32]{1,0:T(8,128)} %constant.20.clone.even_ref, f32[32,32]{1,0:T(8,128)} %constant.21.clone.odd_ref, f32[32,128]{1,0:T(8,128)} %constant.22.clone.xz_ref, f32[64]{0:T(128)} %constant.23.clone.y_ref), custom_call_target="tpu_custom_call" | custom-call | bytes 123136 | tf_op jit(solution)/shard_map/coulomb/pallas_call | solution.py:413
  46.5 1.5 %collective-permute-start.5 = (f32[1,64,128]{2,1,0:T(8,128)}, f32[1,64,128]{2,1,0:T(8,128)S(1)}, u32[]{:S(2)}, u32[]{:S(2)}) collective-permute-start(f32[1,64,128]{2,1,0:T(8,128)} %coulomb.1), channel_id=1, source_target_pairs={{0,4},{1,5},{2,6},{3,7},{4,0},{5,1},{6,2},{7,3},{8,12},{9,13},{10,... | collective-permute-start | bytes 98312 | tf_op jit(solution)/shard_map/ppermute | solution.py:142
  48.0 1.5 %collective-permute-start.16 = (f32[1,64,128]{2,1,0:T(8,128)S(1)}, f32[1,64,128]{2,1,0:T(8,128)S(1)}, u32[]{:S(2)}, u32[]{:S(2)}) collective-permute-start(f32[1,64,128]{2,1,0:T(8,128)S(1)} %fusion.1), channel_id=1, source_target_pairs={{0,4},{1,5},{2,6},{3,7},{4,0},{5,1},{6,2},{7,3},{8,12},{9,13},{10,... | collective-permute-start | bytes 98312 | tf_op jit(solution)/shard_map/ppermute | solution.py:142
  49.6 1.6 %collective-permute-start.27 = (f32[1,64,128]{2,1,0:T(8,128)S(1)}, f32[1,64,128]{2,1,0:T(8,128)S(1)}, u32[]{:S(2)}, u32[]{:S(2)}) collective-permute-start(f32[1,64,128]{2,1,0:T(8,128)S(1)} %fusion), channel_id=1, source_target_pairs={{0,4},{1,5},{2,6},{3,7},{4,0},{5,1},{6,2},{7,3},{8,12},{9,13},{10,... | collective-permute-start | bytes 98312 | tf_op jit(solution)/shard_map/ppermute | solution.py:142
  53.7 1.8 %collective-permute-start.17 = (f32[2,64,128]{2,1,0:T(8,128)S(1)}, f32[2,64,128]{2,1,0:T(8,128)S(1)}, u32[]{:S(2)}, u32[]{:S(2)}) collective-permute-start(f32[2,64,128]{2,1,0:T(8,128)S(1)} %pad_maximum_fusion.7), channel_id=1, source_target_pairs={{0,2},{1,3},{2,0},{3,1},{4,6},{5,7},{6,4},{7,5},{8,10},{9,11},{10,... | collective-permute-start | bytes 196616 | tf_op jit(solution)/shard_map/ppermute | solution.py:142
  58.8 2.1 %collective-permute-start.18 = (f32[4,64,128]{2,1,0:T(8,128)S(1)}, f32[4,64,128]{2,1,0:T(8,128)S(1)}, u32[]{:S(2)}, u32[]{:S(2)}) collective-permute-start(f32[4,64,128]{2,1,0:T(8,128)S(1)} %pad_maximum_fusion.4), channel_id=1, source_target_pairs={{0,1},{1,0},{2,3},{3,2},{4,5},{5,4},{6,7},{7,6},{8,24},{9,25},{10,... | collective-permute-start | bytes 393224 | tf_op jit(solution)/shard_map/ppermute | solution.py:142
  61.3 1.8 %collective-permute-done.7 = f32[4,64,128]{2,1,0:T(8,128)S(1)} collective-permute-done((f32[4,64,128]{2,1,0:T(8,128)S(1)}, f32[4,64,128]{2,1,0:T(8,128)S(1)}, u32[]{:S(2)}, u32[]{:S(2)}) %collective-permute-start.7) | collective-permute-done | bytes 131104 | tf_op jit(solution)/shard_map/ppermute | solution.py:142
  65.1 1.9 %collective-permute-start.19 = (f32[8,64,128]{2,1,0:T(8,128)S(1)}, f32[8,64,128]{2,1,0:T(8,128)S(1)}, u32[]{:S(2)}, u32[]{:S(2)}) collective-permute-start(f32[8,64,128]{2,1,0:T(8,128)S(1)} %pad_maximum_fusion.1.refs_3_), channel_id=1, source_target_pairs={{0,16},{1,17},{2,18},{3,19},{4,20},{5,21},{6,22},{7,23},{8,9},{9,8... | collective-permute-start | bytes 786440 | tf_op jit(solution)/shard_map/ppermute | solution.py:142
  68.2 4.5 %collective-permute-done.8.refs_1_ = f32[8,64,128]{2,1,0:T(8,128)S(1)} collective-permute-done((f32[8,64,128]{2,1,0:T(8,128)S(1)}, f32[8,64,128]{2,1,0:T(8,128)S(1)}, u32[]{:S(2)}, u32[]{:S(2)}) %collective-permute-start.8) | collective-permute-done | bytes 262176 | tf_op jit(solution)/shard_map/ppermute | solution.py:142
  74.9 8.2 %mean.1.refs_1_ = f32[2048,128]{1,0:T(8,128)} custom-call(f32[8,64,128]{2,1,0:T(8,128)} %copy-done.2, f32[8,64,128]{2,1,0:T(8,128)} %copy-done.11, f32[8,64,128]{2,1,0:T(8,128)} %copy-done.10, f32[8,64,128]{2,1,0:T(8,128)} %copy-done.12, f32[2048,128]{1,0:T(8,128)} %bitcast.15, bf16[2,256,256]{2,1,0:T(8,128)(2,1)} %constant.18.clone.refs_5_, ...), custom_call_target="tpu_custom_call" | custom-call | bytes 3801088 | tf_op jit(solution)/shard_map/mean/pallas_call | solution.py:413
  84.1 52.7 %propagate.1 = (f32[8192,128]{1,0:T(8,128)}, f32[3,16,512]{2,1,0:T(8,128)}) custom-call(f32[8192,128]{1,0:T(8,128)} %bitcast.14, f32[2048,128]{1,0:T(8,128)} %mean.1.refs_1_, f32[2048,128]{1,0:T(8,128)} %bitcast.16, f32[8,64,128]{2,1,0:T(8,128)} %copy-done, f32[8,64,128]{2,1,0:T(8,128)} %copy-done.4, f32[8,64,128]{2,1,0:T(8,128)} %copy-done.6, ...), custom_call_target="tpu_custom_call" | custom-call | bytes 12681216 | tf_op jit(solution)/shard_map/propagate/pallas_call | solution.py:413
  (98 shorter events, 21.2 us)
Async XLA Ops:
  9.7 6.5 %collective-permute-start = (f32[16,64,128]{2,1,0:T(8,128)}, f32[16,64,128]{2,1,0:T(8,128)S(1)}, u32[]{:S(2)}, u32[]{:S(2)}) collective-permute-start(f32[16,64,128]{2,1,0:T(8,128)} %get-tuple-element.11), channel_id=1, source_target_pairs={{0,8},{1,9},{2,10},{3,11},{4,12},{5,13},{6,14},{7,15},{8,0},{9,1},... | collective-permute-start | bytes 1572872 | tf_op jit(solution)/shard_map/ppermute | solution.py:126
  15.7 5.9 %collective-permute-start.22 = (f32[16,64,128]{2,1,0:T(8,128)}, f32[16,64,128]{2,1,0:T(8,128)S(1)}, u32[]{:S(2)}, u32[]{:S(2)}) collective-permute-start(f32[16,64,128]{2,1,0:T(8,128)} %get-tuple-element.15), channel_id=1, source_target_pairs={{0,8},{1,9},{2,10},{3,11},{4,12},{5,13},{6,14},{7,15},{8,0},{9,1},... | collective-permute-start | bytes 1572872 | tf_op jit(solution)/shard_map/ppermute | solution.py:126
  16.2 9.6 %collective-permute-start.1 = (f32[8,64,128]{2,1,0:T(8,128)S(1)}, f32[8,64,128]{2,1,0:T(8,128)S(1)}, u32[]{:S(2)}, u32[]{:S(2)}) collective-permute-start(f32[8,64,128]{2,1,0:T(8,128)S(1)} %get-tuple-element.23), channel_id=1, source_target_pairs={{0,2},{1,3},{2,0},{3,1},{4,6},{5,7},{6,4},{7,5},{8,10},{9,11},{10,... | collective-permute-start | bytes 786440 | tf_op jit(solution)/shard_map/ppermute | solution.py:126
  20.0 7.6 %collective-permute-start.12 = (f32[8,64,128]{2,1,0:T(8,128)S(1)}, f32[8,64,128]{2,1,0:T(8,128)S(1)}, u32[]{:S(2)}, u32[]{:S(2)}) collective-permute-start(f32[8,64,128]{2,1,0:T(8,128)S(1)} %get-tuple-element.21), channel_id=1, source_target_pairs={{0,16},{1,17},{2,18},{3,19},{4,20},{5,21},{6,22},{7,23},{8,9},{9,8... | collective-permute-start | bytes 786440 | tf_op jit(solution)/shard_map/ppermute | solution.py:126
  22.7 7.6 %collective-permute-start.23 = (f32[8,64,128]{2,1,0:T(8,128)S(1)}, f32[8,64,128]{2,1,0:T(8,128)S(1)}, u32[]{:S(2)}, u32[]{:S(2)}) collective-permute-start(f32[8,64,128]{2,1,0:T(8,128)S(1)} %get-tuple-element.19), channel_id=1, source_target_pairs={{0,1},{1,0},{2,3},{3,2},{4,5},{5,4},{6,7},{7,6},{8,24},{9,25},{10,... | collective-permute-start | bytes 786440 | tf_op jit(solution)/shard_map/ppermute | solution.py:126
  25.9 6.3 %collective-permute-start.2 = (f32[4,64,128]{2,1,0:T(8,128)S(1)}, f32[4,64,128]{2,1,0:T(8,128)S(1)}, u32[]{:S(2)}, u32[]{:S(2)}) collective-permute-start(f32[4,64,128]{2,1,0:T(8,128)S(1)} %get-tuple-element.29), channel_id=1, source_target_pairs={{0,16},{1,17},{2,18},{3,19},{4,20},{5,21},{6,22},{7,23},{8,9},{9,8... | collective-permute-start | bytes 393224 | tf_op jit(solution)/shard_map/ppermute | solution.py:126
  27.6 6.8 %collective-permute-start.13 = (f32[4,64,128]{2,1,0:T(8,128)S(1)}, f32[4,64,128]{2,1,0:T(8,128)S(1)}, u32[]{:S(2)}, u32[]{:S(2)}) collective-permute-start(f32[4,64,128]{2,1,0:T(8,128)S(1)} %get-tuple-element.27), channel_id=1, source_target_pairs={{0,1},{1,0},{2,3},{3,2},{4,5},{5,4},{6,7},{7,6},{8,24},{9,25},{10,... | collective-permute-start | bytes 393224 | tf_op jit(solution)/shard_map/ppermute | solution.py:126
  34.4 6.0 %collective-permute-start.14 = (f32[2,64,128]{2,1,0:T(8,128)S(1)}, f32[2,64,128]{2,1,0:T(8,128)S(1)}, u32[]{:S(2)}, u32[]{:S(2)}) collective-permute-start(f32[2,64,128]{2,1,0:T(8,128)S(1)} %get-tuple-element.33), channel_id=1, source_target_pairs={{0,2},{1,3},{2,0},{3,1},{4,6},{5,7},{6,4},{7,5},{8,10},{9,11},{10,... | collective-permute-start | bytes 196616 | tf_op jit(solution)/shard_map/ppermute | solution.py:126
  35.6 6.0 %collective-permute-start.25 = (f32[2,64,128]{2,1,0:T(8,128)S(1)}, f32[2,64,128]{2,1,0:T(8,128)S(1)}, u32[]{:S(2)}, u32[]{:S(2)}) collective-permute-start(f32[2,64,128]{2,1,0:T(8,128)S(1)} %get-tuple-element.31), channel_id=1, source_target_pairs={{0,2},{1,3},{2,0},{3,1},{4,6},{5,7},{6,4},{7,5},{8,10},{9,11},{10,... | collective-permute-start | bytes 196616 | tf_op jit(solution)/shard_map/ppermute | solution.py:126
  37.8 6.1 %collective-permute-start.4 = (f32[1,64,128]{2,1,0:T(8,128)S(1)}, f32[1,64,128]{2,1,0:T(8,128)S(1)}, u32[]{:S(2)}, u32[]{:S(2)}) collective-permute-start(f32[1,64,128]{2,1,0:T(8,128)S(1)} %get-tuple-element.36), channel_id=1, source_target_pairs={{0,4},{1,5},{2,6},{3,7},{4,0},{5,1},{6,2},{7,3},{8,12},{9,13},{10,... | collective-permute-start | bytes 98312 | tf_op jit(solution)/shard_map/ppermute | solution.py:126
  40.4 7.7 %collective-permute-start.15 = (f32[1,64,128]{2,1,0:T(8,128)S(1)}, f32[1,64,128]{2,1,0:T(8,128)S(1)}, u32[]{:S(2)}, u32[]{:S(2)}) collective-permute-start(f32[1,64,128]{2,1,0:T(8,128)S(1)} %slice_add_fusion.20), channel_id=1, source_target_pairs={{0,4},{1,5},{2,6},{3,7},{4,0},{5,1},{6,2},{7,3},{8,12},{9,13},{10,... | collective-permute-start | bytes 98312 | tf_op jit(solution)/shard_map/ppermute | solution.py:126
  41.6 7.9 %collective-permute-start.26 = (f32[1,64,128]{2,1,0:T(8,128)S(1)}, f32[1,64,128]{2,1,0:T(8,128)S(1)}, u32[]{:S(2)}, u32[]{:S(2)}) collective-permute-start(f32[1,64,128]{2,1,0:T(8,128)S(1)} %slice_add_fusion.18), channel_id=1, source_target_pairs={{0,4},{1,5},{2,6},{3,7},{4,0},{5,1},{6,2},{7,3},{8,12},{9,13},{10,... | collective-permute-start | bytes 98312 | tf_op jit(solution)/shard_map/ppermute | solution.py:126
  48.0 5.7 %collective-permute-start.16 = (f32[1,64,128]{2,1,0:T(8,128)S(1)}, f32[1,64,128]{2,1,0:T(8,128)S(1)}, u32[]{:S(2)}, u32[]{:S(2)}) collective-permute-start(f32[1,64,128]{2,1,0:T(8,128)S(1)} %fusion.1), channel_id=1, source_target_pairs={{0,4},{1,5},{2,6},{3,7},{4,0},{5,1},{6,2},{7,3},{8,12},{9,13},{10,... | collective-permute-start | bytes 98312 | tf_op jit(solution)/shard_map/ppermute | solution.py:142
  49.6 6.0 %collective-permute-start.27 = (f32[1,64,128]{2,1,0:T(8,128)S(1)}, f32[1,64,128]{2,1,0:T(8,128)S(1)}, u32[]{:S(2)}, u32[]{:S(2)}) collective-permute-start(f32[1,64,128]{2,1,0:T(8,128)S(1)} %fusion), channel_id=1, source_target_pairs={{0,4},{1,5},{2,6},{3,7},{4,0},{5,1},{6,2},{7,3},{8,12},{9,13},{10,... | collective-permute-start | bytes 98312 | tf_op jit(solution)/shard_map/ppermute | solution.py:142
  58.8 6.3 %collective-permute-start.18 = (f32[4,64,128]{2,1,0:T(8,128)S(1)}, f32[4,64,128]{2,1,0:T(8,128)S(1)}, u32[]{:S(2)}, u32[]{:S(2)}) collective-permute-start(f32[4,64,128]{2,1,0:T(8,128)S(1)} %pad_maximum_fusion.4), channel_id=1, source_target_pairs={{0,1},{1,0},{2,3},{3,2},{4,5},{5,4},{6,7},{7,6},{8,24},{9,25},{10,... | collective-permute-start | bytes 393224 | tf_op jit(solution)/shard_map/ppermute | solution.py:142
  60.9 6.1 %collective-permute-start.29 = (f32[4,64,128]{2,1,0:T(8,128)S(1)}, f32[4,64,128]{2,1,0:T(8,128)S(1)}, u32[]{:S(2)}, u32[]{:S(2)}) collective-permute-start(f32[4,64,128]{2,1,0:T(8,128)S(1)} %pad_maximum_fusion.5), channel_id=1, source_target_pairs={{0,16},{1,17},{2,18},{3,19},{4,20},{5,21},{6,22},{7,23},{8,9},{9,8... | collective-permute-start | bytes 393224 | tf_op jit(solution)/shard_map/ppermute | solution.py:142
  63.8 9.3 %collective-permute-start.9 = (f32[8,64,128]{2,1,0:T(8,128)S(1)}, f32[8,64,128]{2,1,0:T(8,128)S(1)}, u32[]{:S(2)}, u32[]{:S(2)}) collective-permute-start(f32[8,64,128]{2,1,0:T(8,128)S(1)} %pad_maximum_fusion.refs_0_), channel_id=1, source_target_pairs={{0,8},{1,9},{2,10},{3,11},{4,12},{5,13},{6,14},{7,15},{8,0},{9,1},... | collective-permute-start | bytes 786440 | tf_op jit(solution)/shard_map/ppermute | solution.py:143
  63.9 8.7 %collective-permute-start.8 = (f32[8,64,128]{2,1,0:T(8,128)S(1)}, f32[8,64,128]{2,1,0:T(8,128)S(1)}, u32[]{:S(2)}, u32[]{:S(2)}) collective-permute-start(f32[8,64,128]{2,1,0:T(8,128)S(1)} %pad_maximum_fusion.refs_0_), channel_id=1, source_target_pairs={{0,2},{1,3},{2,0},{3,1},{4,6},{5,7},{6,4},{7,5},{8,10},{9,11},{10,... | collective-permute-start | bytes 786440 | tf_op jit(solution)/shard_map/ppermute | solution.py:142
  65.1 8.6 %collective-permute-start.19 = (f32[8,64,128]{2,1,0:T(8,128)S(1)}, f32[8,64,128]{2,1,0:T(8,128)S(1)}, u32[]{:S(2)}, u32[]{:S(2)}) collective-permute-start(f32[8,64,128]{2,1,0:T(8,128)S(1)} %pad_maximum_fusion.1.refs_3_), channel_id=1, source_target_pairs={{0,16},{1,17},{2,18},{3,19},{4,20},{5,21},{6,22},{7,23},{8,9},{9,8... | collective-permute-start | bytes 786440 | tf_op jit(solution)/shard_map/ppermute | solution.py:142
  67.0 6.6 %collective-permute-start.30 = (f32[8,64,128]{2,1,0:T(8,128)S(1)}, f32[8,64,128]{2,1,0:T(8,128)S(1)}, u32[]{:S(2)}, u32[]{:S(2)}) collective-permute-start(f32[8,64,128]{2,1,0:T(8,128)S(1)} %pad_maximum_fusion.2.refs_7_), channel_id=1, source_target_pairs={{0,1},{1,0},{2,3},{3,2},{4,5},{5,4},{6,7},{7,6},{8,24},{9,25},{10,... | collective-permute-start | bytes 786440 | tf_op jit(solution)/shard_map/ppermute | solution.py:142
  72.6 10.5 %collective-permute-start.20 = (f32[8,64,128]{2,1,0:T(8,128)S(1)}, f32[8,64,128]{2,1,0:T(8,128)S(1)}, u32[]{:S(2)}, u32[]{:S(2)}) collective-permute-start(f32[8,64,128]{2,1,0:T(8,128)S(1)} %pad_maximum_fusion.1.refs_3_), channel_id=1, source_target_pairs={{0,8},{1,9},{2,10},{3,11},{4,12},{5,13},{6,14},{7,15},{8,0},{9,1},... | collective-permute-start | bytes 786440 | tf_op jit(solution)/shard_map/ppermute | solution.py:143
  73.1 10.0 %collective-permute-start.31 = (f32[8,64,128]{2,1,0:T(8,128)S(1)}, f32[8,64,128]{2,1,0:T(8,128)S(1)}, u32[]{:S(2)}, u32[]{:S(2)}) collective-permute-start(f32[8,64,128]{2,1,0:T(8,128)S(1)} %pad_maximum_fusion.2.refs_7_), channel_id=1, source_target_pairs={{0,8},{1,9},{2,10},{3,11},{4,12},{5,13},{6,14},{7,15},{8,0},{9,1},... | collective-permute-start | bytes 786440 | tf_op jit(solution)/shard_map/ppermute | solution.py:143
  73.6 9.5 %collective-permute-start.21 = (f32[8,64,128]{2,1,0:T(8,128)S(1)}, f32[8,64,128]{2,1,0:T(8,128)S(1)}, u32[]{:S(2)}, u32[]{:S(2)}) collective-permute-start(f32[8,64,128]{2,1,0:T(8,128)S(1)} %collective-permute-done.19.refs_4_), channel_id=1, source_target_pairs={{0,8},{1,9},{2,10},{3,11},{4,12},{5,13},{6,14},{7,15},{8,0},{9,1},... | collective-permute-start | bytes 786440 | tf_op jit(solution)/shard_map/ppermute | solution.py:143
  73.7 9.5 %collective-permute-start.32 = (f32[8,64,128]{2,1,0:T(8,128)S(1)}, f32[8,64,128]{2,1,0:T(8,128)S(1)}, u32[]{:S(2)}, u32[]{:S(2)}) collective-permute-start(f32[8,64,128]{2,1,0:T(8,128)S(1)} %collective-permute-done.30.refs_8_), channel_id=1, source_target_pairs={{0,8},{1,9},{2,10},{3,11},{4,12},{5,13},{6,14},{7,15},{8,0},{9,1},... | collective-permute-start | bytes 786440 | tf_op jit(solution)/shard_map/ppermute | solution.py:143
  (23 other events, 118.0 us)

commit v2 on v1

v2 whole, which is shorter than its diff:
```python
import functools
import math

import jax
import jax.numpy as jnp
import numpy as np
from jax import lax
from jax.experimental import pallas as pl
from jax.experimental.pallas import tpu as pltpu
from jax.sharding import PartitionSpec as P

NX = 64
NG = 64
LANES = 2 * NG
PLANE = NG * NG // LANES
ROWS = NX * PLANE
AXES = ("grp", "wf")
GROUP = 4
ODD_AT = PLANE + 16
PADDED = ODD_AT + PLANE

time_step = 0.2
kinetic_coef = 0.5
density_coef = 1.0
coulomb_coef = 0.25

F32 = jnp.float32
BF16 = jnp.bfloat16


def fourier_basis(length):
    cells = np.arange(length)
    rows, waves = [np.ones(length) / math.sqrt(length)], [0]
    for wave in range(1, length // 2):
        angle = 2.0 * math.pi * (wave * cells % length) / length
        rows += [math.sqrt(2.0 / length) * np.cos(angle), math.sqrt(2.0 / length) * np.sin(angle)]
        waves += [wave, wave]
    rows.append(np.where(cells % 2 == 0, 1.0, -1.0) / math.sqrt(length))
    waves.append(length // 2)
    return np.stack(rows), np.array(waves)


def lattice_symbol(waves, length):
    return 2.0 - 2.0 * np.cos(2.0 * math.pi / length * waves)


def split(matrix):
    high = matrix.astype(np.float32).astype(jnp.bfloat16)
    low = (matrix - high.astype(np.float64)).astype(jnp.bfloat16)
    return np.stack([high, low])


def block_diagonal(matrix, count):
    return np.kron(np.eye(count), matrix)


def transform_tables():
    basis, waves = fourier_basis(NG)
    order = np.concatenate([np.arange(0, NG, 2), np.arange(1, NG, 2)])
    forward_y = block_diagonal(basis[:, order], GROUP)
    forward_z = block_diagonal(basis.T, 2)
    first, first_waves = fourier_basis(NX)
    even, odd = first_waves % 2 == 0, first_waves % 2 == 1
    symbol_x = lattice_symbol(first_waves, NX)
    symbol = lattice_symbol(waves, NG)
    symbol_xz = np.concatenate(
        [symbol_x[even][:, None] + symbol[None], symbol_x[odd][:, None] + symbol[None]], axis=1
    )
    ring = np.roll(np.eye(NG), 1, axis=1) + np.roll(np.eye(NG), -1, axis=1)
    depth = block_diagonal(ring, 2)
    return dict(
        depth=np.concatenate([depth, depth]).astype(jnp.bfloat16),
        forward_y=split(forward_y),
        forward_z=split(forward_z),
        inverse_y=split(forward_y.T),
        inverse_z=split(forward_z.T),
        even=first[even][:, : NX // 2].astype(np.float32),
        odd=first[odd][:, : NX // 2].astype(np.float32),
        symbol_xz=symbol_xz.astype(np.float32),
        symbol_y=symbol.astype(np.float32),
    )


class Plan:
    def __init__(self, sizes, orders, pieces):
        self.sizes = sizes
        self.orders = orders
        self.pieces = pieces
        self.halvings = int(math.log2(pieces)) - 1
        kept = [("grp", 1)] + sorted(orders[0][: self.halvings])
        assert kept[1:] == sorted(orders[1][: self.halvings])
        self.kept = kept

    def permutation(self, step):
        pairs = []
        for grp in range(self.sizes["grp"]):
            for wf in range(self.sizes["wf"]):
                axis, mask = ("grp", 1) if step < 0 else self.orders[grp & 1][step]
                to = (grp ^ mask, wf) if axis == "grp" else (grp, wf ^ mask)
                pairs.append((grp * self.sizes["wf"] + wf, to[0] * self.sizes["wf"] + to[1]))
        return pairs

    def identity(self, grp, wf):
        number = 0
        for place, (axis, mask) in enumerate(self.kept):
            value = grp if axis == "grp" else wf
            number = number + (((value >> int(math.log2(mask))) & 1) << place)
        return number

    def places(self, side):
        grp, wf = lax.axis_index("grp"), lax.axis_index("wf")
        core = (grp & 1) ^ side
        pieces = [self.identity(grp ^ side, wf)]
        for step in range(self.halvings):
            near, far = (
                self.identity(*[mask if axis == name else 0 for name in AXES])
                for axis, mask in (self.orders[0][step], self.orders[1][step])
            )
            flip = near + core * (far - near)
            pieces = [piece ^ turned for piece in pieces for turned in (0, flip)]
        return pieces


def reduce_scatter(plan, own, other):
    for step in range(-1, len(plan.orders[0])):
        received = lax.ppermute(other, AXES, plan.permutation(step))
        if step + 1 == len(plan.orders[0]):
            break
        if step + 1 < plan.halvings:
            half = own.shape[0] // 2
            own, other = own[:half] + received[:half], own[half:] + received[half:]
        else:
            own = own + received
            other = own
    return own, received


def all_gather(plan, piece):
    parts = [piece]
    for step in reversed(range(plan.halvings)):
        whole = parts[0] if len(parts) == 1 else jnp.concatenate(parts)
        parts = [whole, lax.ppermute(whole, AXES, plan.permutation(step))]
    return parts + [lax.ppermute(part, AXES, plan.permutation(-1)) for part in parts]


def lane(shape):
    return lax.broadcasted_iota(jnp.int32, shape, len(shape) - 1)


def swap(value):
    return pltpu.roll(value, NG, value.ndim - 1)


def cut(value):
    high = value.astype(BF16)
    return high, (value - high.astype(F32)).astype(BF16)


def product(left, right):
    return lax.dot_general(left, right, (((1,), (0,)), ((), ())), preferred_element_type=F32)


def times_table(value, table):
    high, low = cut(value)
    return product(high, table[0]) + (product(low, table[0]) + product(high, table[1]))


def table_times(table, value):
    high, low = cut(value)
    return product(table[0], high) + (product(table[0], low) + product(table[1], high))


def component(state_ref, wave, index, row, rows):
    return state_ref[pl.ds((wave * ROWS + row) * 4 + index, rows, stride=4), :]


def fold(near, far):
    low = lane(near.shape) < NG
    return jnp.where(low, near, swap(far)), jnp.where(low, swap(near), far)


def unfold(even, odd):
    low = lane(even.shape) < NG
    return jnp.where(low, even, swap(odd)), jnp.where(low, swap(even), odd)


def deal(plan, whole_ref, own_ref, other_ref):
    rows = ROWS // plan.pieces
    for side, out_ref in enumerate((own_ref, other_ref)):
        for index, piece in enumerate(plan.places(side)):
            out_ref[index] = whole_ref[pl.ds(pl.multiple_of(piece * rows, 8), rows), :]


def collect(plan, part_refs, whole_ref):
    rows = ROWS // plan.pieces
    for side in range(2):
        for index, piece in enumerate(plan.places(side)):
            part, at = divmod(index, plan.pieces // 4)
            whole_ref[pl.ds(pl.multiple_of(piece * rows, 8), rows), :] = part_refs[2 * side + part][at]


def kappa_kernel(plans, waves, scale, state_ref, *refs):
    out_refs, whole_refs = refs[:4], refs[4:]

    def kappa(plane):
        real = imag = None
        for wave in range(waves):
            u_real, u_imag, v_real, v_imag = (component(state_ref, wave, c, plane * PLANE, PLANE) for c in range(4))
            add_real = u_real * v_real + u_imag * v_imag
            add_imag = u_imag * v_real - u_real * v_imag
            real = add_real if real is None else real + add_real
            imag = add_imag if imag is None else imag + add_imag
        return real * scale, imag * scale

    def body(plane, carry):
        base = pl.multiple_of(plane * NG, 8)
        for near, far, whole_ref in zip(kappa(plane), kappa(plane + NX // 2), whole_refs):
            even, odd = fold(near, far)
            whole_ref[pl.ds(base, PLANE), :] = even
            whole_ref[pl.ds(base + PLANE, PLANE), :] = odd
        return carry

    lax.fori_loop(0, NX // 2, body, 0)
    for which, plan in enumerate(plans):
        deal(plan, whole_refs[which], out_refs[2 * which], out_refs[2 * which + 1])


def density_kernel(plan, waves, scale, state_ref, y_ref, z_ref, own_ref, other_ref, spectrum_ref):
    half = NX // 2

    def density(plane):
        total = None
        for wave in range(waves):
            real = component(state_ref, wave, 2, plane * PLANE, PLANE)
            imag = component(state_ref, wave, 3, plane * PLANE, PLANE)
            value = real * real + imag * imag
            total = value if total is None else total + value
        return total * scale

    def body(pair, carry):
        for group in (2 * pair, 2 * pair + 1):
            parts = []
            for j in range(GROUP):
                plane = group * GROUP + j
                parts += fold(density(plane), density(plane + half))
            value = times_table(jnp.concatenate(parts), z_ref)
            value = table_times(y_ref, value)
            for j in range(GROUP):
                spectrum_ref[pl.ds(group * GROUP + j, NG, stride=half), :] = value[j * NG : (j + 1) * NG]
        return carry

    lax.fori_loop(0, half // GROUP // 2, body, 0)
    deal(plan, spectrum_ref, own_ref, other_ref)


def coulomb_kernel(plan, own_ref, received_ref, even_ref, odd_ref, xz_ref, y_ref, out_ref):
    half = NX // 2
    low_lanes = lane((half, LANES)) < NG
    sign = jnp.where(low_lanes, 1.0, -1.0)
    count = ROWS // plan.pieces // half
    first = plan.identity(lax.axis_index("grp"), lax.axis_index("wf")) * count

    def dot(matrix, value, axis):
        return lax.dot_general(
            matrix, value, (((axis,), (0,)), ((), ())),
            precision=lax.Precision.HIGHEST, preferred_element_type=F32,
        )

    for k in range(count):
        rows = pl.ds(k * half, half)
        value = own_ref[0, rows, :] + received_ref[0, rows, :]
        value = swap(value) + sign * value
        value = jnp.where(low_lanes, dot(even_ref[...], value, 1), dot(odd_ref[...], value, 1))
        squared = xz_ref[...] + y_ref[first + k]
        kernel = jnp.where(
            squared > 0.001,
            4.0 * math.pi * coulomb_coef / jnp.where(squared > 0.001, squared, 1.0),
            0.0,
        )
        value = value * (density_coef + kernel)
        value = jnp.where(low_lanes, dot(even_ref[...], value, 0), dot(odd_ref[...], value, 0))
        out_ref[0, rows, :] = swap(value) + sign * value


def mean_kernel(plan, *refs):
    part_refs, (outer_ref, y_ref, z_ref, out_ref, spectrum_ref) = refs[:4], refs[4:]
    half = NX // 2
    collect(plan, part_refs, spectrum_ref)

    def body(pair, carry):
        for group in (2 * pair, 2 * pair + 1):
            value = jnp.concatenate(
                [spectrum_ref[pl.ds(group * GROUP + j, NG, stride=half), :] for j in range(GROUP)]
            )
            value = table_times(y_ref, value)
            value = times_table(value, z_ref)
            for j in range(GROUP):
                plane = group * GROUP + j
                near, far = (
                    outer_ref[pl.ds(pl.multiple_of(x * PLANE, 8), PLANE), :] for x in (plane, plane + half)
                )
                base = pl.multiple_of(plane * NG, 8)
                for part, outer in enumerate(fold(near, far)):
                    at = j * NG + part * PLANE
                    out_ref[pl.ds(base + part * PLANE, PLANE), :] = value[at : at + PLANE] + outer
        return carry

    lax.fori_loop(0, half // GROUP // 2, body, 0)


def propagate_kernel(plans, *refs):
    (state_ref, mean_ref, coupling_ref, depth_ref), refs = refs[:4], refs[4:]
    parts, refs = (refs[:4], refs[4:8]), refs[8:]
    out_ref, potentials_ref, single_ref, real_ref, imag_ref, depth_sum_ref = refs[:6]
    term_refs = refs[6:]
    half = NX // 2

    for plan, part_refs, pair_ref in zip(plans, parts, (real_ref, imag_ref)):
        collect(plan, part_refs, pair_ref)

    def write(ref, c, plane, part, chunk, value):
        base = pl.multiple_of((plane + 1) * PADDED, 8)
        if part == 0:
            ref[c, pl.ds(base + chunk * 8, 8), :] = value
            if chunk == 0:
                ref[c, pl.ds(base + PLANE, 1), :] = value[:1]
        else:
            ref[c, pl.ds(base + ODD_AT + chunk * 8, 8), :] = value
            if chunk == PLANE // 8 - 1:
                ref[c, pl.ds(base + ODD_AT - 1, 1), :] = value[7:]

    def close(ref):
        for source, target in ((0, half + 1), (half - 1, 0)):
            for c in range(4):
                for at in (0, ODD_AT):
                    value = ref[c, pl.ds((source + 1) * PADDED + at, PLANE), :]
                    ref[c, pl.ds(target * PADDED + at, PLANE), :] = swap(value)

    def prepare(plane, carry):
        for chunk in range(PLANE // 8):
            rows = [pl.multiple_of(x * PLANE + chunk * 8, 8) for x in (plane, plane + half)]
            folded = fold(*[coupling_ref[pl.ds(row, 8), :] for row in rows])
            for part in range(2):
                where = pl.ds(pl.multiple_of(plane * NG + part * PLANE + chunk * 8, 8), 8)
                single_ref[where, :] = 2.0 * mean_ref[where, :] + 12.0 * kinetic_coef
                real_ref[where, :] = -2.0 * folded[part] * real_ref[where, :]
                imag_ref[where, :] = -2.0 * folded[part] * imag_ref[where, :]
            for c in range(4):
                folded = fold(*[component(state_ref, 0, c, row, 8) for row in rows])
                for part in range(2):
                    write(term_refs[0], c, plane, part, chunk, folded[part])
        return carry

    lax.fori_loop(0, half, prepare, 0)
    close(term_refs[0])

    planes, width = potentials_ref.shape[1:]
    first = lax.axis_index("grp") * planes
    upper = first >= half
    start = (first - jnp.where(upper, half, 0)) * NG + lax.axis_index("wf") * (width // LANES)
    low = lane((planes, LANES)) < NG
    for which, (ref, factor) in enumerate(((mean_ref, 1.0), (real_ref, 0.5), (imag_ref, 0.5))):
        for j in range(width // LANES):
            even = ref[pl.ds(start + j, planes, stride=NG), :]
            odd = ref[pl.ds(start + PLANE + j, planes, stride=NG), :]
            near, far = unfold(even, odd)
            potentials_ref[which, :, j * LANES : (j + 1) * LANES] = factor * jnp.where(upper, far, near)

    def depth_sums(source, plane, slot):
        base = pl.multiple_of((plane + 1) * PADDED, 8)
        value = jnp.concatenate([source[c, pl.ds(base + at, PLANE), :] for c in range(4) for at in (0, ODD_AT)])
        depth_sum_ref[slot] = product(jnp.concatenate(cut(value), axis=1), depth_ref[...])

    def finish(source, target, plane, slot):
        base = pl.multiple_of((plane + 1) * PADDED, 8)
        for part in range(2):
            for chunk in range(PLANE // 8):
                at = chunk * 8 + part * ODD_AT
                across = chunk * 8 + (1 - part) * ODD_AT
                beyond = across - 1 if part == 0 else across + 1
                where = pl.ds(pl.multiple_of(plane * NG + part * PLANE + chunk * 8, 8), 8)
                single, real, imag = single_ref[where, :], real_ref[where, :], imag_ref[where, :]
                state, total = [], []
                for c in range(4):
                    state.append(source[c, pl.ds(base + at, 8), :])
                    total.append(
                        (source[c, pl.ds(base - PADDED + at, 8), :] + source[c, pl.ds(base + PADDED + at, 8), :])
                        + (source[c, pl.ds(base + across, 8), :] + source[c, pl.ds(base + beyond, 8), :])
                        + depth_sum_ref[slot, pl.ds(c * NG + part * PLANE + chunk * 8, 8), :]
                    )
                values = (
                    (single * state[1] - total[1]) + (real * state[3] + imag * state[2]),
                    (total[0] - single * state[0]) + (imag * state[3] - real * state[2]),
                    (total[3] - single * state[3]) + (real * state[1] - imag * state[0]),
                    (single * state[2] - total[2]) - (real * state[0] + imag * state[1]),
                )
                if target is not None:
                    for c in range(4):
                        write(target, c, plane, part, chunk, values[c])
                    continue
                for c in range(4):
                    result = values[c] * weights[4] + state[c] * weights[3]
                    for k in (2, 1):
                        result = result + term_refs[k][c, pl.ds(base + at, 8), :] * weights[k]
                    results[part][chunk][c] = result + term_refs[0][c, pl.ds(base + at, 8), :]
        if target is None:
            for chunk in range(PLANE // 8):
                for c in range(4):
                    folded = unfold(results[0][chunk][c], results[1][chunk][c])
                    for x, value in zip((plane, plane + half), folded):
                        out_ref[pl.ds((x * PLANE + chunk * 8) * 4 + c, 8, stride=4), :] = value

    weights = [(0.5 * time_step) ** k / math.factorial(k) for k in range(5)]
    results = [[[None] * 4 for _ in range(PLANE // 8)] for _ in range(2)]
    for source, target in zip(term_refs, list(term_refs[1:]) + [None]):
        depth_sums(source, 0, 0)

        def body(pair, carry, source=source, target=target):
            for slot in range(2):
                finish(source, target, 2 * pair + slot, slot)
                depth_sums(source, 2 * pair + slot + 1, 1 - slot)
            return carry

        lax.fori_loop(0, half // 2, body, 0)
        if target is not None:
            close(target)


def vmem(count):
    return [pl.BlockSpec(memory_space=pltpu.VMEM)] * count


def call(kernel, name, out_shapes, operands, scratch=(), in_specs=None, flops=0):
    moved = sum(math.prod(o.shape) * 4 for o in out_shapes) + sum(math.prod(o.shape) * 4 for o in operands)
    return pl.pallas_call(
        kernel,
        name=name,
        out_shape=[jax.ShapeDtypeStruct(o.shape, o.dtype) for o in out_shapes],
        in_specs=in_specs or vmem(len(operands)),
        out_specs=vmem(len(out_shapes)),
        scratch_shapes=[pltpu.VMEM(shape, F32) for shape in scratch],
        compiler_params=pltpu.CompilerParams(vmem_limit_bytes=56 * 1024 * 1024),
        cost_estimate=pl.CostEstimate(flops=flops, bytes_accessed=moved, transcendentals=0),
    )(*operands)


def like(*shape):
    return jax.ShapeDtypeStruct(shape, F32)


def local(quasi, outer_field, coupling):
    sizes = {name: lax.axis_size(name) for name in AXES}
    devices = sizes["grp"] * sizes["wf"]
    waves = quasi.shape[0]
    scale = 1.0 / (waves * devices)
    bits = [("grp", 1 << k) for k in range(1, sizes["grp"].bit_length() - 1)]
    bits += [("wf", 1 << k) for k in range(sizes["wf"].bit_length() - 1)]
    first, second, third, rest = bits[0], bits[1], bits[2], bits[3:]
    straight = [first, second, third] + rest
    crossed = [second, first, third] + rest
    real_plan = Plan(sizes, (straight, crossed), devices)
    imag_plan = Plan(sizes, (crossed, straight), devices)
    mean_plan = Plan(sizes, ([third, first, second] + rest, [third, second, first] + rest), min(devices, NG))
    tables = {name: jnp.asarray(table) for name, table in transform_tables().items()}

    def halves(plan):
        return [like(plan.pieces // 2, ROWS // plan.pieces, LANES)] * 2

    state = quasi.reshape(waves, 4, ROWS, LANES).transpose(0, 2, 1, 3).reshape(waves * ROWS * 4, LANES)
    outer_field = outer_field.reshape(ROWS, LANES)
    coupling = coupling.reshape(ROWS, LANES)

    real_own, real_other, imag_own, imag_other = call(
        functools.partial(kappa_kernel, (real_plan, imag_plan), waves, scale),
        "kappa", halves(real_plan) + halves(imag_plan), [state], [(ROWS, LANES)] * 2,
    )
    mean_own, mean_other = call(
        functools.partial(density_kernel, mean_plan, waves, scale),
        "density", halves(mean_plan), [state, tables["forward_y"], tables["forward_z"]], [(ROWS, LANES)],
    )
    real = reduce_scatter(real_plan, real_own, real_other)
    imag = reduce_scatter(imag_plan, imag_own, imag_other)
    mean = reduce_scatter(mean_plan, mean_own, mean_other)
    (spectrum,) = call(
        functools.partial(coulomb_kernel, mean_plan),
        "coulomb", [like(*mean[0].shape)],
        [*mean, tables["even"], tables["odd"], tables["symbol_xz"], tables["symbol_y"]],
        in_specs=vmem(5) + [pl.BlockSpec(memory_space=pltpu.SMEM)],
    )
    mean_parts = all_gather(mean_plan, spectrum)
    real_parts = all_gather(real_plan, real[0] + real[1])
    imag_parts = all_gather(imag_plan, imag[0] + imag[1])
    (mean_field,) = call(
        functools.partial(mean_kernel, mean_plan),
        "mean", [like(ROWS, LANES)],
        [*mean_parts, outer_field, tables["inverse_y"], tables["inverse_z"]], [(ROWS, LANES)],
    )

    padded = (4, (NX // 2 + 2) * PADDED, LANES)
    evolved = []
    for wave in range(waves):
        own_state = state[wave * ROWS * 4 : (wave + 1) * ROWS * 4]
        evolved_rows, potentials = call(
            functools.partial(propagate_kernel, (real_plan, imag_plan)),
            "propagate",
            [like(ROWS * 4, LANES), like(3, NX // sizes["grp"], NG * NG // sizes["wf"])],
            [own_state, mean_field, coupling, tables["depth"], *real_parts, *imag_parts],
            [(ROWS, LANES)] * 3 + [(2, 4 * NG, LANES)] + [padded] * 4,
        )
        evolved.append(evolved_rows)
    evolved = jnp.concatenate(evolved) if waves > 1 else evolved[0]
    evolved = evolved.reshape(waves, ROWS, 4, LANES).transpose(0, 2, 1, 3).reshape(quasi.shape)
    return (evolved, potentials)


def solution(mesh):
    placed = (P(AXES, None, None), P(), P())
    return jax.shard_map(
        local,
        mesh=mesh,
        in_specs=placed,
        out_specs=(P(AXES, None, None), P(None, "grp", "wf")),
        check_vma=False,
    )
```

time: 137 us -> 108 us (0.79)
  Pallas kernels: 77.6 us -> 47.8 us
    pallas_call x5, Pallas kernels: 77.6 us -> 47.8 us  [call(): pl.pallas_call(kernel, name=name, out_shape=[jax.ShapeDtypeStruct(o.shape...]
  transfers between devices with their start and end apart: 33 -> 33, of which waited for: 9 -> 9; matrix products, arithmetic and copies ran while one was open for 4% -> 5% of each run, Pallas kernels for 12% -> 14%
where the time goes in v2:
time: 108 us; the launch traced here: 107 us
  Pallas kernels  47.8 us (44%)
  starting transfers between devices  39.3 us (36%)
  waiting for transfers between devices  11.4 us (11%)
  other arithmetic  5.44 us (5%)
  local copies, waits for them, and re-layouts  2.23 us (2%)
    pallas_call x5, Pallas kernels, call(): pl.pallas_call(kernel, name=name, out_shape=[jax.ShapeDtypeStruct(o.shape...  47.8 us
    ppermute x15, starting transfers between devices, reduce_scatter(): received = lax.ppermute(other, AXES, plan.permutation(step))  22.5 us
    ppermute x12, starting transfers between devices, all_gather(): parts = [whole, lax.ppermute(whole, AXES, plan.permutation(step))]  15.7 us
    ppermute x12, waiting for transfers between devices, all_gather(): parts = [whole, lax.ppermute(whole, AXES, plan.permutation(step))]  8.3 us
    ppermute x15, waiting for transfers between devices, reduce_scatter(): received = lax.ppermute(other, AXES, plan.permutation(step))  3.11 us
    add x12, other arithmetic, reduce_scatter(): own, other = (own[:half] + received[:half], own[half:] + received[half:])  3.04 us
    concatenate x9, other arithmetic, all_gather(): whole = parts[0] if len(parts) == 1 else jnp.concatenate(parts)  2.38 us
    unnamed x28, local copies, waits for them, and re-layouts  2.23 us
  transfers between devices with their start and end apart: 33, of which 9 were waited for; matrix products, arithmetic and copies ran while one was open for 5% of the time, Pallas kernels for 14%

profile of v2, /device:TPU:0, one launch (start us, length us, event | category | flops | bytes accessed | tf_op | source)
XLA Modules:
  0.0 107.0 jit_solution(11562607641490830663)
XLA Ops:
  0.6 7.5 %density.1 = (f32[16,64,128]{2,1,0:T(8,128)}, f32[16,64,128]{2,1,0:T(8,128)}) custom-call(f32[8192,128]{1,0:T(8,128)} %bitcast.12, bf16[2,256,256]{2,1,0:T(8,128)(2,1)} %constant.19.clone.y_ref, bf16[2,128,128]{2,1,0:T(8,128)(2,1)} %constant.20.clone.z_ref), custom_call_target="tpu_custom_call" | custom-call | bytes 5898240 | tf_op jit(solution)/shard_map/density/pallas_call | solution.py:435
  8.6 6.5 %kappa.1 = (f32[16,64,128]{2,1,0:T(8,128)}, f32[16,64,128]{2,1,0:T(8,128)}, f32[16,64,128]{2,1,0:T(8,128)}, f32[16,64,128]{2,1,0:T(8,128)}) custom-call(f32[8192,128]{1,0:T(8,128)} %bitcast.13), custom_call_target="tpu_custom_call" | custom-call | bytes 6291456 | tf_op jit(solution)/shard_map/kappa/pallas_call | solution.py:435
  15.6 2.7 %collective-permute-start.1 = (f32[8,64,128]{2,1,0:T(8,128)S(1)}, f32[8,64,128]{2,1,0:T(8,128)S(1)}, u32[]{:S(2)}, u32[]{:S(2)}) collective-permute-start(f32[8,64,128]{2,1,0:T(8,128)S(1)} %get-tuple-element.23), channel_id=1, source_target_pairs={{0,2},{1,3},{2,0},{3,1},{4,6},{5,7},{6,4},{7,5},{8,10},{9,11},{10,... | collective-permute-start | bytes 786440 | tf_op jit(solution)/shard_map/ppermute | solution.py:126
  19.4 1.6 %collective-permute-start.12 = (f32[8,64,128]{2,1,0:T(8,128)S(1)}, f32[8,64,128]{2,1,0:T(8,128)S(1)}, u32[]{:S(2)}, u32[]{:S(2)}) collective-permute-start(f32[8,64,128]{2,1,0:T(8,128)S(1)} %get-tuple-element.21), channel_id=1, source_target_pairs={{0,16},{1,17},{2,18},{3,19},{4,20},{5,21},{6,22},{7,23},{8,9},{9,8... | collective-permute-start | bytes 786440 | tf_op jit(solution)/shard_map/ppermute | solution.py:126
  22.1 1.6 %collective-permute-start.23 = (f32[8,64,128]{2,1,0:T(8,128)S(1)}, f32[8,64,128]{2,1,0:T(8,128)S(1)}, u32[]{:S(2)}, u32[]{:S(2)}) collective-permute-start(f32[8,64,128]{2,1,0:T(8,128)S(1)} %get-tuple-element.19), channel_id=1, source_target_pairs={{0,1},{1,0},{2,3},{3,2},{4,5},{5,4},{6,7},{7,6},{8,24},{9,25},{10,... | collective-permute-start | bytes 786440 | tf_op jit(solution)/shard_map/ppermute | solution.py:126
  23.7 1.5 %collective-permute-done.1 = f32[8,64,128]{2,1,0:T(8,128)S(1)} collective-permute-done((f32[8,64,128]{2,1,0:T(8,128)S(1)}, f32[8,64,128]{2,1,0:T(8,128)S(1)}, u32[]{:S(2)}, u32[]{:S(2)}) %collective-permute-start.1) | collective-permute-done | bytes 262176 | tf_op jit(solution)/shard_map/ppermute | solution.py:126
  25.3 1.7 %collective-permute-start.2 = (f32[4,64,128]{2,1,0:T(8,128)S(1)}, f32[4,64,128]{2,1,0:T(8,128)S(1)}, u32[]{:S(2)}, u32[]{:S(2)}) collective-permute-start(f32[4,64,128]{2,1,0:T(8,128)S(1)} %get-tuple-element.29), channel_id=1, source_target_pairs={{0,16},{1,17},{2,18},{3,19},{4,20},{5,21},{6,22},{7,23},{8,9},{9,8... | collective-permute-start | bytes 393224 | tf_op jit(solution)/shard_map/ppermute | solution.py:126
  27.0 2.7 %collective-permute-start.13 = (f32[4,64,128]{2,1,0:T(8,128)S(1)}, f32[4,64,128]{2,1,0:T(8,128)S(1)}, u32[]{:S(2)}, u32[]{:S(2)}) collective-permute-start(f32[4,64,128]{2,1,0:T(8,128)S(1)} %get-tuple-element.27), channel_id=1, source_target_pairs={{0,1},{1,0},{2,3},{3,2},{4,5},{5,4},{6,7},{7,6},{8,24},{9,25},{10,... | collective-permute-start | bytes 393224 | tf_op jit(solution)/shard_map/ppermute | solution.py:126
  29.7 1.4 %collective-permute-start.24 = (f32[4,64,128]{2,1,0:T(8,128)S(1)}, f32[4,64,128]{2,1,0:T(8,128)S(1)}, u32[]{:S(2)}, u32[]{:S(2)}) collective-permute-start(f32[4,64,128]{2,1,0:T(8,128)S(1)} %get-tuple-element.25), channel_id=1, source_target_pairs={{0,16},{1,17},{2,18},{3,19},{4,20},{5,21},{6,22},{7,23},{8,9},{9,8... | collective-permute-start | bytes 393224 | tf_op jit(solution)/shard_map/ppermute | solution.py:126
  31.6 1.5 %collective-permute-start.3 = (f32[2,64,128]{2,1,0:T(8,128)S(1)}, f32[2,64,128]{2,1,0:T(8,128)S(1)}, u32[]{:S(2)}, u32[]{:S(2)}) collective-permute-start(f32[2,64,128]{2,1,0:T(8,128)S(1)} %get-tuple-element.35), channel_id=1, source_target_pairs={{0,1},{1,0},{2,3},{3,2},{4,5},{5,4},{6,7},{7,6},{8,24},{9,25},{10,... | collective-permute-start | bytes 196616 | tf_op jit(solution)/shard_map/ppermute | solution.py:126
  35.0 1.5 %collective-permute-start.25 = (f32[2,64,128]{2,1,0:T(8,128)S(1)}, f32[2,64,128]{2,1,0:T(8,128)S(1)}, u32[]{:S(2)}, u32[]{:S(2)}) collective-permute-start(f32[2,64,128]{2,1,0:T(8,128)S(1)} %get-tuple-element.31), channel_id=1, source_target_pairs={{0,2},{1,3},{2,0},{3,1},{4,6},{5,7},{6,4},{7,5},{8,10},{9,11},{10,... | collective-permute-start | bytes 196616 | tf_op jit(solution)/shard_map/ppermute | solution.py:126
  37.2 2.6 %collective-permute-start.4 = (f32[1,64,128]{2,1,0:T(8,128)S(1)}, f32[1,64,128]{2,1,0:T(8,128)S(1)}, u32[]{:S(2)}, u32[]{:S(2)}) collective-permute-start(f32[1,64,128]{2,1,0:T(8,128)S(1)} %get-tuple-element.36), channel_id=1, source_target_pairs={{0,4},{1,5},{2,6},{3,7},{4,0},{5,1},{6,2},{7,3},{8,12},{9,13},{10,... | collective-permute-start | bytes 98312 | tf_op jit(solution)/shard_map/ppermute | solution.py:126
  41.0 1.8 %collective-permute-start.26 = (f32[1,64,128]{2,1,0:T(8,128)S(1)}, f32[1,64,128]{2,1,0:T(8,128)S(1)}, u32[]{:S(2)}, u32[]{:S(2)}) collective-permute-start(f32[1,64,128]{2,1,0:T(8,128)S(1)} %slice_add_fusion.18), channel_id=1, source_target_pairs={{0,4},{1,5},{2,6},{3,7},{4,0},{5,1},{6,2},{7,3},{8,12},{9,13},{10,... | collective-permute-start | bytes 98312 | tf_op jit(solution)/shard_map/ppermute | solution.py:126
  43.9 2.1 %coulomb.1 = f32[1,64,128]{2,1,0:T(8,128)} custom-call(f32[1,64,128]{2,1,0:T(8,128)} %get-tuple-element.37.own_ref, f32[1,64,128]{2,1,0:T(8,128)} %copy-done.13, f32[32,32]{1,0:T(8,128)} %constant.23.clone.even_ref, f32[32,32]{1,0:T(8,128)} %constant.24.clone.odd_ref, f32[32,128]{1,0:T(8,128)} %constant.25.clone.xz_ref, f32[64]{0:T(128)} %constant.26.clone.y_ref), custom_call_target="tpu_custom_call" | custom-call | bytes 123136 | tf_op jit(solution)/shard_map/coulomb/pallas_call | solution.py:435
  45.9 1.5 %collective-permute-start.5 = (f32[1,64,128]{2,1,0:T(8,128)}, f32[1,64,128]{2,1,0:T(8,128)S(1)}, u32[]{:S(2)}, u32[]{:S(2)}) collective-permute-start(f32[1,64,128]{2,1,0:T(8,128)} %coulomb.1), channel_id=1, source_target_pairs={{0,4},{1,5},{2,6},{3,7},{4,0},{5,1},{6,2},{7,3},{8,12},{9,13},{10,... | collective-permute-start | bytes 98312 | tf_op jit(solution)/shard_map/ppermute | solution.py:142
  47.5 1.5 %collective-permute-start.16 = (f32[1,64,128]{2,1,0:T(8,128)S(1)}, f32[1,64,128]{2,1,0:T(8,128)S(1)}, u32[]{:S(2)}, u32[]{:S(2)}) collective-permute-start(f32[1,64,128]{2,1,0:T(8,128)S(1)} %fusion.1), channel_id=1, source_target_pairs={{0,4},{1,5},{2,6},{3,7},{4,0},{5,1},{6,2},{7,3},{8,12},{9,13},{10,... | collective-permute-start | bytes 98312 | tf_op jit(solution)/shard_map/ppermute | solution.py:142
  49.0 1.6 %collective-permute-start.27 = (f32[1,64,128]{2,1,0:T(8,128)S(1)}, f32[1,64,128]{2,1,0:T(8,128)S(1)}, u32[]{:S(2)}, u32[]{:S(2)}) collective-permute-start(f32[1,64,128]{2,1,0:T(8,128)S(1)} %fusion), channel_id=1, source_target_pairs={{0,4},{1,5},{2,6},{3,7},{4,0},{5,1},{6,2},{7,3},{8,12},{9,13},{10,... | collective-permute-start | bytes 98312 | tf_op jit(solution)/shard_map/ppermute | solution.py:142
  53.1 1.8 %collective-permute-start.17 = (f32[2,64,128]{2,1,0:T(8,128)S(1)}, f32[2,64,128]{2,1,0:T(8,128)S(1)}, u32[]{:S(2)}, u32[]{:S(2)}) collective-permute-start(f32[2,64,128]{2,1,0:T(8,128)S(1)} %pad_maximum_fusion.7), channel_id=1, source_target_pairs={{0,2},{1,3},{2,0},{3,1},{4,6},{5,7},{6,4},{7,5},{8,10},{9,11},{10,... | collective-permute-start | bytes 196616 | tf_op jit(solution)/shard_map/ppermute | solution.py:142
  58.2 2.2 %collective-permute-start.18 = (f32[4,64,128]{2,1,0:T(8,128)S(1)}, f32[4,64,128]{2,1,0:T(8,128)S(1)}, u32[]{:S(2)}, u32[]{:S(2)}) collective-permute-start(f32[4,64,128]{2,1,0:T(8,128)S(1)} %pad_maximum_fusion.4), channel_id=1, source_target_pairs={{0,1},{1,0},{2,3},{3,2},{4,5},{5,4},{6,7},{7,6},{8,24},{9,25},{10,... | collective-permute-start | bytes 393224 | tf_op jit(solution)/shard_map/ppermute | solution.py:142
  60.7 1.8 %collective-permute-done.7 = f32[4,64,128]{2,1,0:T(8,128)S(1)} collective-permute-done((f32[4,64,128]{2,1,0:T(8,128)S(1)}, f32[4,64,128]{2,1,0:T(8,128)S(1)}, u32[]{:S(2)}, u32[]{:S(2)}) %collective-permute-start.7) | collective-permute-done | bytes 131104 | tf_op jit(solution)/shard_map/ppermute | solution.py:142
  64.5 1.9 %collective-permute-start.19 = (f32[8,64,128]{2,1,0:T(8,128)S(1)}, f32[8,64,128]{2,1,0:T(8,128)S(1)}, u32[]{:S(2)}, u32[]{:S(2)}) collective-permute-start(f32[8,64,128]{2,1,0:T(8,128)S(1)} %pad_maximum_fusion.1.refs_4_), channel_id=1, source_target_pairs={{0,16},{1,17},{2,18},{3,19},{4,20},{5,21},{6,22},{7,23},{8,9},{9,8... | collective-permute-start | bytes 786440 | tf_op jit(solution)/shard_map/ppermute | solution.py:142
  67.6 4.4 %collective-permute-done.8.refs_1_ = f32[8,64,128]{2,1,0:T(8,128)S(1)} collective-permute-done((f32[8,64,128]{2,1,0:T(8,128)S(1)}, f32[8,64,128]{2,1,0:T(8,128)S(1)}, u32[]{:S(2)}, u32[]{:S(2)}) %collective-permute-start.8) | collective-permute-done | bytes 262176 | tf_op jit(solution)/shard_map/ppermute | solution.py:142
  74.3 6.0 %mean.1.refs_1_ = f32[2048,128]{1,0:T(8,128)} custom-call(f32[8,64,128]{2,1,0:T(8,128)} %copy-done.2, f32[8,64,128]{2,1,0:T(8,128)} %copy-done.11, f32[8,64,128]{2,1,0:T(8,128)} %copy-done.10, f32[8,64,128]{2,1,0:T(8,128)} %copy-done.12, f32[2048,128]{1,0:T(8,128)} %bitcast.15, bf16[2,256,256]{2,1,0:T(8,128)(2,1)} %constant.21.clone.refs_5_, ...), custom_call_target="tpu_custom_call" | custom-call | bytes 3801088 | tf_op jit(solution)/shard_map/mean/pallas_call | solution.py:435
  81.3 25.7 %propagate.1 = (f32[8192,128]{1,0:T(8,128)}, f32[3,16,512]{2,1,0:T(8,128)}) custom-call(f32[8192,128]{1,0:T(8,128)} %bitcast.14, f32[2048,128]{1,0:T(8,128)} %mean.1.refs_1_, f32[2048,128]{1,0:T(8,128)} %bitcast.16, bf16[256,128]{1,0:T(8,128)(2,1)} %constant.18.clone.refs_3_, f32[8,64,128]{2,1,0:T(8,128)} %copy-done, f32[8,64,128]{2,1,0:T(8,128)} %copy-done.4, ...), custom_call_target="tpu_custom_call" | custom-call | bytes 12812288 | tf_op jit(solution)/shard_map/propagate/pallas_call | solution.py:435
  (98 shorter events, 21.1 us)
Async XLA Ops:
  8.1 7.5 %collective-permute-start = (f32[16,64,128]{2,1,0:T(8,128)}, f32[16,64,128]{2,1,0:T(8,128)S(1)}, u32[]{:S(2)}, u32[]{:S(2)}) collective-permute-start(f32[16,64,128]{2,1,0:T(8,128)} %get-tuple-element.11), channel_id=1, source_target_pairs={{0,8},{1,9},{2,10},{3,11},{4,12},{5,13},{6,14},{7,15},{8,0},{9,1},... | collective-permute-start | bytes 1572872 | tf_op jit(solution)/shard_map/ppermute | solution.py:126
  15.1 5.9 %collective-permute-start.22 = (f32[16,64,128]{2,1,0:T(8,128)}, f32[16,64,128]{2,1,0:T(8,128)S(1)}, u32[]{:S(2)}, u32[]{:S(2)}) collective-permute-start(f32[16,64,128]{2,1,0:T(8,128)} %get-tuple-element.15), channel_id=1, source_target_pairs={{0,8},{1,9},{2,10},{3,11},{4,12},{5,13},{6,14},{7,15},{8,0},{9,1},... | collective-permute-start | bytes 1572872 | tf_op jit(solution)/shard_map/ppermute | solution.py:126
  15.6 9.6 %collective-permute-start.1 = (f32[8,64,128]{2,1,0:T(8,128)S(1)}, f32[8,64,128]{2,1,0:T(8,128)S(1)}, u32[]{:S(2)}, u32[]{:S(2)}) collective-permute-start(f32[8,64,128]{2,1,0:T(8,128)S(1)} %get-tuple-element.23), channel_id=1, source_target_pairs={{0,2},{1,3},{2,0},{3,1},{4,6},{5,7},{6,4},{7,5},{8,10},{9,11},{10,... | collective-permute-start | bytes 786440 | tf_op jit(solution)/shard_map/ppermute | solution.py:126
  19.4 7.6 %collective-permute-start.12 = (f32[8,64,128]{2,1,0:T(8,128)S(1)}, f32[8,64,128]{2,1,0:T(8,128)S(1)}, u32[]{:S(2)}, u32[]{:S(2)}) collective-permute-start(f32[8,64,128]{2,1,0:T(8,128)S(1)} %get-tuple-element.21), channel_id=1, source_target_pairs={{0,16},{1,17},{2,18},{3,19},{4,20},{5,21},{6,22},{7,23},{8,9},{9,8... | collective-permute-start | bytes 786440 | tf_op jit(solution)/shard_map/ppermute | solution.py:126
  22.1 7.6 %collective-permute-start.23 = (f32[8,64,128]{2,1,0:T(8,128)S(1)}, f32[8,64,128]{2,1,0:T(8,128)S(1)}, u32[]{:S(2)}, u32[]{:S(2)}) collective-permute-start(f32[8,64,128]{2,1,0:T(8,128)S(1)} %get-tuple-element.19), channel_id=1, source_target_pairs={{0,1},{1,0},{2,3},{3,2},{4,5},{5,4},{6,7},{7,6},{8,24},{9,25},{10,... | collective-permute-start | bytes 786440 | tf_op jit(solution)/shard_map/ppermute | solution.py:126
  25.3 6.3 %collective-permute-start.2 = (f32[4,64,128]{2,1,0:T(8,128)S(1)}, f32[4,64,128]{2,1,0:T(8,128)S(1)}, u32[]{:S(2)}, u32[]{:S(2)}) collective-permute-start(f32[4,64,128]{2,1,0:T(8,128)S(1)} %get-tuple-element.29), channel_id=1, source_target_pairs={{0,16},{1,17},{2,18},{3,19},{4,20},{5,21},{6,22},{7,23},{8,9},{9,8... | collective-permute-start | bytes 393224 | tf_op jit(solution)/shard_map/ppermute | solution.py:126
  27.0 6.7 %collective-permute-start.13 = (f32[4,64,128]{2,1,0:T(8,128)S(1)}, f32[4,64,128]{2,1,0:T(8,128)S(1)}, u32[]{:S(2)}, u32[]{:S(2)}) collective-permute-start(f32[4,64,128]{2,1,0:T(8,128)S(1)} %get-tuple-element.27), channel_id=1, source_target_pairs={{0,1},{1,0},{2,3},{3,2},{4,5},{5,4},{6,7},{7,6},{8,24},{9,25},{10,... | collective-permute-start | bytes 393224 | tf_op jit(solution)/shard_map/ppermute | solution.py:126
  33.8 6.0 %collective-permute-start.14 = (f32[2,64,128]{2,1,0:T(8,128)S(1)}, f32[2,64,128]{2,1,0:T(8,128)S(1)}, u32[]{:S(2)}, u32[]{:S(2)}) collective-permute-start(f32[2,64,128]{2,1,0:T(8,128)S(1)} %get-tuple-element.33), channel_id=1, source_target_pairs={{0,2},{1,3},{2,0},{3,1},{4,6},{5,7},{6,4},{7,5},{8,10},{9,11},{10,... | collective-permute-start | bytes 196616 | tf_op jit(solution)/shard_map/ppermute | solution.py:126
  35.0 6.0 %collective-permute-start.25 = (f32[2,64,128]{2,1,0:T(8,128)S(1)}, f32[2,64,128]{2,1,0:T(8,128)S(1)}, u32[]{:S(2)}, u32[]{:S(2)}) collective-permute-start(f32[2,64,128]{2,1,0:T(8,128)S(1)} %get-tuple-element.31), channel_id=1, source_target_pairs={{0,2},{1,3},{2,0},{3,1},{4,6},{5,7},{6,4},{7,5},{8,10},{9,11},{10,... | collective-permute-start | bytes 196616 | tf_op jit(solution)/shard_map/ppermute | solution.py:126
  37.2 6.1 %collective-permute-start.4 = (f32[1,64,128]{2,1,0:T(8,128)S(1)}, f32[1,64,128]{2,1,0:T(8,128)S(1)}, u32[]{:S(2)}, u32[]{:S(2)}) collective-permute-start(f32[1,64,128]{2,1,0:T(8,128)S(1)} %get-tuple-element.36), channel_id=1, source_target_pairs={{0,4},{1,5},{2,6},{3,7},{4,0},{5,1},{6,2},{7,3},{8,12},{9,13},{10,... | collective-permute-start | bytes 98312 | tf_op jit(solution)/shard_map/ppermute | solution.py:126
  39.8 7.7 %collective-permute-start.15 = (f32[1,64,128]{2,1,0:T(8,128)S(1)}, f32[1,64,128]{2,1,0:T(8,128)S(1)}, u32[]{:S(2)}, u32[]{:S(2)}) collective-permute-start(f32[1,64,128]{2,1,0:T(8,128)S(1)} %slice_add_fusion.20), channel_id=1, source_target_pairs={{0,4},{1,5},{2,6},{3,7},{4,0},{5,1},{6,2},{7,3},{8,12},{9,13},{10,... | collective-permute-start | bytes 98312 | tf_op jit(solution)/shard_map/ppermute | solution.py:126
  41.0 7.9 %collective-permute-start.26 = (f32[1,64,128]{2,1,0:T(8,128)S(1)}, f32[1,64,128]{2,1,0:T(8,128)S(1)}, u32[]{:S(2)}, u32[]{:S(2)}) collective-permute-start(f32[1,64,128]{2,1,0:T(8,128)S(1)} %slice_add_fusion.18), channel_id=1, source_target_pairs={{0,4},{1,5},{2,6},{3,7},{4,0},{5,1},{6,2},{7,3},{8,12},{9,13},{10,... | collective-permute-start | bytes 98312 | tf_op jit(solution)/shard_map/ppermute | solution.py:126
  47.5 5.7 %collective-permute-start.16 = (f32[1,64,128]{2,1,0:T(8,128)S(1)}, f32[1,64,128]{2,1,0:T(8,128)S(1)}, u32[]{:S(2)}, u32[]{:S(2)}) collective-permute-start(f32[1,64,128]{2,1,0:T(8,128)S(1)} %fusion.1), channel_id=1, source_target_pairs={{0,4},{1,5},{2,6},{3,7},{4,0},{5,1},{6,2},{7,3},{8,12},{9,13},{10,... | collective-permute-start | bytes 98312 | tf_op jit(solution)/shard_map/ppermute | solution.py:142
  49.0 6.0 %collective-permute-start.27 = (f32[1,64,128]{2,1,0:T(8,128)S(1)}, f32[1,64,128]{2,1,0:T(8,128)S(1)}, u32[]{:S(2)}, u32[]{:S(2)}) collective-permute-start(f32[1,64,128]{2,1,0:T(8,128)S(1)} %fusion), channel_id=1, source_target_pairs={{0,4},{1,5},{2,6},{3,7},{4,0},{5,1},{6,2},{7,3},{8,12},{9,13},{10,... | collective-permute-start | bytes 98312 | tf_op jit(solution)/shard_map/ppermute | solution.py:142
  58.2 6.3 %collective-permute-start.18 = (f32[4,64,128]{2,1,0:T(8,128)S(1)}, f32[4,64,128]{2,1,0:T(8,128)S(1)}, u32[]{:S(2)}, u32[]{:S(2)}) collective-permute-start(f32[4,64,128]{2,1,0:T(8,128)S(1)} %pad_maximum_fusion.4), channel_id=1, source_target_pairs={{0,1},{1,0},{2,3},{3,2},{4,5},{5,4},{6,7},{7,6},{8,24},{9,25},{10,... | collective-permute-start | bytes 393224 | tf_op jit(solution)/shard_map/ppermute | solution.py:142
  60.4 6.1 %collective-permute-start.29 = (f32[4,64,128]{2,1,0:T(8,128)S(1)}, f32[4,64,128]{2,1,0:T(8,128)S(1)}, u32[]{:S(2)}, u32[]{:S(2)}) collective-permute-start(f32[4,64,128]{2,1,0:T(8,128)S(1)} %pad_maximum_fusion.5), channel_id=1, source_target_pairs={{0,16},{1,17},{2,18},{3,19},{4,20},{5,21},{6,22},{7,23},{8,9},{9,8... | collective-permute-start | bytes 393224 | tf_op jit(solution)/shard_map/ppermute | solution.py:142
  63.2 9.3 %collective-permute-start.9 = (f32[8,64,128]{2,1,0:T(8,128)S(1)}, f32[8,64,128]{2,1,0:T(8,128)S(1)}, u32[]{:S(2)}, u32[]{:S(2)}) collective-permute-start(f32[8,64,128]{2,1,0:T(8,128)S(1)} %pad_maximum_fusion.refs_0_), channel_id=1, source_target_pairs={{0,8},{1,9},{2,10},{3,11},{4,12},{5,13},{6,14},{7,15},{8,0},{9,1},... | collective-permute-start | bytes 786440 | tf_op jit(solution)/shard_map/ppermute | solution.py:143
  63.3 8.7 %collective-permute-start.8 = (f32[8,64,128]{2,1,0:T(8,128)S(1)}, f32[8,64,128]{2,1,0:T(8,128)S(1)}, u32[]{:S(2)}, u32[]{:S(2)}) collective-permute-start(f32[8,64,128]{2,1,0:T(8,128)S(1)} %pad_maximum_fusion.refs_0_), channel_id=1, source_target_pairs={{0,2},{1,3},{2,0},{3,1},{4,6},{5,7},{6,4},{7,5},{8,10},{9,11},{10,... | collective-permute-start | bytes 786440 | tf_op jit(solution)/shard_map/ppermute | solution.py:142
  64.5 8.6 %collective-permute-start.19 = (f32[8,64,128]{2,1,0:T(8,128)S(1)}, f32[8,64,128]{2,1,0:T(8,128)S(1)}, u32[]{:S(2)}, u32[]{:S(2)}) collective-permute-start(f32[8,64,128]{2,1,0:T(8,128)S(1)} %pad_maximum_fusion.1.refs_4_), channel_id=1, source_target_pairs={{0,16},{1,17},{2,18},{3,19},{4,20},{5,21},{6,22},{7,23},{8,9},{9,8... | collective-permute-start | bytes 786440 | tf_op jit(solution)/shard_map/ppermute | solution.py:142
  66.5 6.6 %collective-permute-start.30 = (f32[8,64,128]{2,1,0:T(8,128)S(1)}, f32[8,64,128]{2,1,0:T(8,128)S(1)}, u32[]{:S(2)}, u32[]{:S(2)}) collective-permute-start(f32[8,64,128]{2,1,0:T(8,128)S(1)} %pad_maximum_fusion.2.refs_8_), channel_id=1, source_target_pairs={{0,1},{1,0},{2,3},{3,2},{4,5},{5,4},{6,7},{7,6},{8,24},{9,25},{10,... | collective-permute-start | bytes 786440 | tf_op jit(solution)/shard_map/ppermute | solution.py:142
  72.0 8.3 %collective-permute-start.20 = (f32[8,64,128]{2,1,0:T(8,128)S(1)}, f32[8,64,128]{2,1,0:T(8,128)S(1)}, u32[]{:S(2)}, u32[]{:S(2)}) collective-permute-start(f32[8,64,128]{2,1,0:T(8,128)S(1)} %pad_maximum_fusion.1.refs_4_), channel_id=1, source_target_pairs={{0,8},{1,9},{2,10},{3,11},{4,12},{5,13},{6,14},{7,15},{8,0},{9,1},... | collective-permute-start | bytes 786440 | tf_op jit(solution)/shard_map/ppermute | solution.py:143
  72.5 7.8 %collective-permute-start.31 = (f32[8,64,128]{2,1,0:T(8,128)S(1)}, f32[8,64,128]{2,1,0:T(8,128)S(1)}, u32[]{:S(2)}, u32[]{:S(2)}) collective-permute-start(f32[8,64,128]{2,1,0:T(8,128)S(1)} %pad_maximum_fusion.2.refs_8_), channel_id=1, source_target_pairs={{0,8},{1,9},{2,10},{3,11},{4,12},{5,13},{6,14},{7,15},{8,0},{9,1},... | collective-permute-start | bytes 786440 | tf_op jit(solution)/shard_map/ppermute | solution.py:143
  73.1 7.3 %collective-permute-start.21 = (f32[8,64,128]{2,1,0:T(8,128)S(1)}, f32[8,64,128]{2,1,0:T(8,128)S(1)}, u32[]{:S(2)}, u32[]{:S(2)}) collective-permute-start(f32[8,64,128]{2,1,0:T(8,128)S(1)} %collective-permute-done.19.refs_5_), channel_id=1, source_target_pairs={{0,8},{1,9},{2,10},{3,11},{4,12},{5,13},{6,14},{7,15},{8,0},{9,1},... | collective-permute-start | bytes 786440 | tf_op jit(solution)/shard_map/ppermute | solution.py:143
  73.1 7.3 %collective-permute-start.32 = (f32[8,64,128]{2,1,0:T(8,128)S(1)}, f32[8,64,128]{2,1,0:T(8,128)S(1)}, u32[]{:S(2)}, u32[]{:S(2)}) collective-permute-start(f32[8,64,128]{2,1,0:T(8,128)S(1)} %collective-permute-done.30.refs_9_), channel_id=1, source_target_pairs={{0,8},{1,9},{2,10},{3,11},{4,12},{5,13},{6,14},{7,15},{8,0},{9,1},... | collective-permute-start | bytes 786440 | tf_op jit(solution)/shard_map/ppermute | solution.py:143
  (23 other events, 110.1 us)

commit v3 on v2

v3 whole, which is shorter than its diff:
```python
import functools
import math

import jax
import jax.numpy as jnp
import numpy as np
from jax import lax
from jax.experimental import pallas as pl
from jax.experimental.pallas import tpu as pltpu
from jax.sharding import PartitionSpec as P

NX = 64
NG = 64
LANES = 2 * NG
PLANE = NG * NG // LANES
ROWS = NX * PLANE
AXES = ("grp", "wf")
GROUP = 4
PAD = 8
PADDED = PLANE + 2 * PAD
STEP = 2
CHUNKS = 8

time_step = 0.2
kinetic_coef = 0.5
density_coef = 1.0
coulomb_coef = 0.25

F32 = jnp.float32
BF16 = jnp.bfloat16


def fourier_basis(length):
    cells = np.arange(length)
    rows, waves = [np.ones(length) / math.sqrt(length)], [0]
    for wave in range(1, length // 2):
        angle = 2.0 * math.pi * (wave * cells % length) / length
        rows += [math.sqrt(2.0 / length) * np.cos(angle), math.sqrt(2.0 / length) * np.sin(angle)]
        waves += [wave, wave]
    rows.append(np.where(cells % 2 == 0, 1.0, -1.0) / math.sqrt(length))
    waves.append(length // 2)
    return np.stack(rows), np.array(waves)


def lattice_symbol(waves, length):
    return 2.0 - 2.0 * np.cos(2.0 * math.pi / length * waves)


def split(matrix):
    high = matrix.astype(np.float32).astype(jnp.bfloat16)
    low = (matrix - high.astype(np.float64)).astype(jnp.bfloat16)
    return np.stack([high, low])


def block_diagonal(matrix, count):
    return np.kron(np.eye(count), matrix)


def transform_tables():
    basis, waves = fourier_basis(NG)
    order = np.concatenate([np.arange(0, NG, 2), np.arange(1, NG, 2)])
    forward_y = block_diagonal(basis[:, order], GROUP)
    forward_z = block_diagonal(basis.T, 2)
    first, first_waves = fourier_basis(NX)
    even, odd = first_waves % 2 == 0, first_waves % 2 == 1
    symbol_x = lattice_symbol(first_waves, NX)
    symbol = lattice_symbol(waves, NG)
    symbol_xz = np.concatenate(
        [symbol_x[even][:, None] + symbol[None], symbol_x[odd][:, None] + symbol[None]], axis=1
    )
    ring = np.roll(np.eye(NG), 1, axis=1) + np.roll(np.eye(NG), -1, axis=1)
    swapped = np.roll(np.eye(LANES), NG, axis=1)
    shift = np.concatenate([block_diagonal(ring, 2) + swapped, swapped], axis=1)
    return dict(
        shift=np.concatenate([shift, shift]).astype(jnp.bfloat16),
        forward_y=split(forward_y),
        forward_z=split(forward_z),
        inverse_y=split(forward_y.T),
        inverse_z=split(forward_z.T),
        even=first[even][:, : NX // 2].astype(np.float32),
        odd=first[odd][:, : NX // 2].astype(np.float32),
        symbol_xz=symbol_xz.astype(np.float32),
        symbol_y=symbol.astype(np.float32),
    )


class Plan:
    def __init__(self, sizes, orders, pieces):
        self.sizes = sizes
        self.orders = orders
        self.pieces = pieces
        self.halvings = int(math.log2(pieces)) - 1
        kept = [("grp", 1)] + sorted(orders[0][: self.halvings])
        assert kept[1:] == sorted(orders[1][: self.halvings])
        self.kept = kept

    def permutation(self, step):
        pairs = []
        for grp in range(self.sizes["grp"]):
            for wf in range(self.sizes["wf"]):
                axis, mask = ("grp", 1) if step < 0 else self.orders[grp & 1][step]
                to = (grp ^ mask, wf) if axis == "grp" else (grp, wf ^ mask)
                pairs.append((grp * self.sizes["wf"] + wf, to[0] * self.sizes["wf"] + to[1]))
        return pairs

    def identity(self, grp, wf):
        number = 0
        for place, (axis, mask) in enumerate(self.kept):
            value = grp if axis == "grp" else wf
            number = number + (((value >> int(math.log2(mask))) & 1) << place)
        return number

    def places(self, side):
        grp, wf = lax.axis_index("grp"), lax.axis_index("wf")
        core = (grp & 1) ^ side
        pieces = [self.identity(grp ^ side, wf)]
        for step in range(self.halvings):
            near, far = (
                self.identity(*[mask if axis == name else 0 for name in AXES])
                for axis, mask in (self.orders[0][step], self.orders[1][step])
            )
            flip = near + core * (far - near)
            pieces = [piece ^ turned for piece in pieces for turned in (0, flip)]
        return pieces


def reduce_scatter(plan, own, other):
    for step in range(-1, len(plan.orders[0])):
        received = lax.ppermute(other, AXES, plan.permutation(step))
        if step + 1 == len(plan.orders[0]):
            break
        if step + 1 < plan.halvings:
            half = own.shape[0] // 2
            own, other = own[:half] + received[:half], own[half:] + received[half:]
        else:
            own = own + received
            other = own
    return own, received


def all_gather(plan, piece):
    parts = [piece]
    for step in reversed(range(plan.halvings)):
        whole = parts[0] if len(parts) == 1 else jnp.concatenate(parts)
        parts = [whole, lax.ppermute(whole, AXES, plan.permutation(step))]
    return parts + [lax.ppermute(part, AXES, plan.permutation(-1)) for part in parts]


def lane(shape):
    return lax.broadcasted_iota(jnp.int32, shape, len(shape) - 1)


def swap(value):
    return pltpu.roll(value, NG, value.ndim - 1)


def cut(value):
    high = value.astype(BF16)
    return high, (value - high.astype(F32)).astype(BF16)


def product(left, right):
    return lax.dot_general(left, right, (((1,), (0,)), ((), ())), preferred_element_type=F32)


def times_table(value, table):
    high, low = cut(value)
    return product(high, table[0]) + (product(low, table[0]) + product(high, table[1]))


def table_times(table, value):
    high, low = cut(value)
    return product(table[0], high) + (product(table[0], low) + product(table[1], high))


def fold(near, far):
    low = lane(near.shape) < NG
    return jnp.where(low, near, swap(far)), jnp.where(low, swap(near), far)


def unfold(even, odd):
    low = lane(even.shape) < NG
    return jnp.where(low, even, swap(odd)), jnp.where(low, swap(even), odd)


def deal(plan, whole_ref, own_ref, other_ref):
    rows = ROWS // plan.pieces
    for side, out_ref in enumerate((own_ref, other_ref)):
        for index, piece in enumerate(plan.places(side)):
            out_ref[index] = whole_ref[pl.ds(pl.multiple_of(piece * rows, 8), rows), :]


def collect(plan, part_refs, store):
    rows = ROWS // plan.pieces
    for side in range(2):
        for index, piece in enumerate(plan.places(side)):
            part, at = divmod(index, plan.pieces // 4)
            store(pl.ds(pl.multiple_of(piece * rows, 8), rows), part_refs[2 * side + part][at])


def kappa_kernel(plans, scale, state_ref, *refs):
    out_refs, psi_ref, whole_refs, arrived = refs[:4], refs[4], refs[5:7], refs[7]
    waves, rows = psi_ref.shape[0], ROWS // CHUNKS
    copies = [
        [
            pltpu.make_async_copy(
                state_ref.at[wave, pl.ds(chunk * rows, rows), c, :],
                psi_ref.at[wave, c, pl.ds(chunk * rows, rows), :],
                arrived.at[chunk, wave, c],
            )
            for wave in range(waves)
            for c in range(4)
        ]
        for chunk in range(CHUNKS)
    ]
    for chunk in copies:
        for copy in chunk:
            copy.start()

    for chunk in range(CHUNKS):
        for copy in copies[chunk]:
            copy.wait()

        def body(plane, carry, chunk=chunk):
            where = pl.ds(pl.multiple_of(chunk * rows + plane * PLANE, 8), PLANE)
            real = imag = None
            for wave in range(waves):
                u_real, u_imag, v_real, v_imag = (psi_ref[wave, c, where, :] for c in range(4))
                add_real = u_real * v_real + u_imag * v_imag
                add_imag = u_imag * v_real - u_real * v_imag
                real = add_real if real is None else real + add_real
                imag = add_imag if imag is None else imag + add_imag
            whole_refs[0][where, :] = real * scale
            whole_refs[1][where, :] = imag * scale
            return carry

        lax.fori_loop(0, rows // PLANE, body, 0)
    for which, plan in enumerate(plans):
        deal(plan, whole_refs[which], out_refs[2 * which], out_refs[2 * which + 1])


def density_kernel(plan, scale, psi_ref, y_ref, z_ref, own_ref, other_ref, spectrum_ref):
    half = NX // 2

    def density(plane):
        where = pl.ds(pl.multiple_of(plane * PLANE, 8), PLANE)
        total = None
        for wave in range(psi_ref.shape[0]):
            real, imag = psi_ref[wave, 2, where, :], psi_ref[wave, 3, where, :]
            value = real * real + imag * imag
            total = value if total is None else total + value
        return total * scale

    def body(pair, carry):
        for group in (2 * pair, 2 * pair + 1):
            parts = []
            for j in range(GROUP):
                plane = group * GROUP + j
                parts += fold(density(plane), density(plane + half))
            value = times_table(jnp.concatenate(parts), z_ref)
            value = table_times(y_ref, value)
            for j in range(GROUP):
                spectrum_ref[pl.ds(group * GROUP + j, NG, stride=half), :] = value[j * NG : (j + 1) * NG]
        return carry

    lax.fori_loop(0, half // GROUP // 2, body, 0)
    deal(plan, spectrum_ref, own_ref, other_ref)


def coulomb_kernel(plan, own_ref, received_ref, even_ref, odd_ref, xz_ref, y_ref, out_ref):
    half = NX // 2
    low_lanes = lane((half, LANES)) < NG
    sign = jnp.where(low_lanes, 1.0, -1.0)
    count = ROWS // plan.pieces // half
    first = plan.identity(lax.axis_index("grp"), lax.axis_index("wf")) * count

    def dot(matrix, value, axis):
        return lax.dot_general(
            matrix, value, (((axis,), (0,)), ((), ())),
            precision=lax.Precision.HIGHEST, preferred_element_type=F32,
        )

    for k in range(count):
        rows = pl.ds(k * half, half)
        value = own_ref[0, rows, :] + received_ref[0, rows, :]
        value = swap(value) + sign * value
        value = jnp.where(low_lanes, dot(even_ref[...], value, 1), dot(odd_ref[...], value, 1))
        squared = xz_ref[...] + y_ref[first + k]
        kernel = jnp.where(
            squared > 0.001,
            4.0 * math.pi * coulomb_coef / jnp.where(squared > 0.001, squared, 1.0),
            0.0,
        )
        value = value * (density_coef + kernel)
        value = jnp.where(low_lanes, dot(even_ref[...], value, 0), dot(odd_ref[...], value, 0))
        out_ref[0, rows, :] = swap(value) + sign * value


def mean_kernel(plan, *refs):
    part_refs, (outer_ref, y_ref, z_ref, out_ref, spectrum_ref) = refs[:4], refs[4:]
    half = NX // 2

    def store(where, value):
        spectrum_ref[where, :] = value

    collect(plan, part_refs, store)

    def body(pair, carry):
        for group in (2 * pair, 2 * pair + 1):
            value = jnp.concatenate(
                [spectrum_ref[pl.ds(group * GROUP + j, NG, stride=half), :] for j in range(GROUP)]
            )
            value = table_times(y_ref, value)
            value = times_table(value, z_ref)
            for j in range(GROUP):
                at = j * NG
                natural = unfold(value[at : at + PLANE], value[at + PLANE : at + NG])
                for x, part in zip((group * GROUP + j, group * GROUP + j + half), natural):
                    where = pl.ds(pl.multiple_of(x * PLANE, 8), PLANE)
                    out_ref[where, :] = part + outer_ref[where, :]
        return carry

    lax.fori_loop(0, half // GROUP // 2, body, 0)


def propagate_kernel(plans, *refs):
    (psi_ref, mean_ref, coupling_ref, shift_ref), refs = refs[:4], refs[4:]
    parts, refs = (refs[:4], refs[4:8]), refs[8:]
    out_ref, potentials_ref, single_ref, real_ref, imag_ref, inner_ref, swapped_ref = refs[:7]
    (*buffers, left) = refs[7:]
    terms = [psi_ref.at[0]] + buffers

    for plan, part_refs, pair_ref in zip(plans, parts, (real_ref, imag_ref)):

        def store(where, value, pair_ref=pair_ref):
            pair_ref[where, :] = -2.0 * coupling_ref[where, :] * value

        collect(plan, part_refs, store)

    def prepare(plane, carry):
        where = pl.ds(pl.multiple_of(plane * PLANE, 8), PLANE)
        single_ref[where, :] = 2.0 * mean_ref[where, :] + 12.0 * kinetic_coef
        return carry

    lax.fori_loop(0, NX, prepare, 0)

    planes, width = potentials_ref.shape[1:]
    start = lax.axis_index("grp") * planes * PLANE + lax.axis_index("wf") * (width // LANES)
    for which, (ref, factor) in enumerate(((mean_ref, 1.0), (real_ref, 0.5), (imag_ref, 0.5))):
        for j in range(width // LANES):
            value = ref[pl.ds(start + j, planes, stride=PLANE), :]
            potentials_ref[which, :, j * LANES : (j + 1) * LANES] = factor * value

    low_lanes = lane((8, LANES)) < NG

    def in_lanes(source, first, slot):
        value = jnp.concatenate(
            [
                source[c, pl.ds(pl.multiple_of((first + p) * PLANE, 8), PLANE), :]
                for p in range(STEP)
                for c in range(4)
            ]
        )
        moved = product(jnp.concatenate(cut(value), axis=1), shift_ref[...])
        inner_ref[slot] = moved[:, :LANES]
        for k in range(4 * STEP):
            rows = moved[k * PLANE : (k + 1) * PLANE, LANES:]
            swapped_ref[slot, k, PAD : PAD + PLANE] = rows
            swapped_ref[slot, k, PAD - 1 : PAD] = rows[PLANE - 1 :]
            swapped_ref[slot, k, PAD + PLANE : PAD + PLANE + 1] = rows[:1]

    weights = [(0.5 * time_step) ** k / math.factorial(k) for k in range(5)]

    def finish(source, target, plane, p, slot):
        base = pl.multiple_of(plane * PLANE, 8)
        before = pl.multiple_of(((plane + NX - 1) & (NX - 1)) * PLANE, 8)
        after = pl.multiple_of(((plane + 1) & (NX - 1)) * PLANE, 8)
        for chunk in range(PLANE // 8):
            where = pl.ds(base + chunk * 8, 8)
            single, real, imag = single_ref[where, :], real_ref[where, :], imag_ref[where, :]
            state, total = [], []
            for c in range(4):
                k = p * 4 + c
                at = PAD + chunk * 8
                state.append(source[c, where, :])
                total.append(
                    (source[c, pl.ds(before + chunk * 8, 8), :] + source[c, pl.ds(after + chunk * 8, 8), :])
                    + (
                        inner_ref[slot, k * PLANE + chunk * 8 : k * PLANE + chunk * 8 + 8]
                        + jnp.where(
                            low_lanes,
                            swapped_ref[slot, k, at - 1 : at + 7],
                            swapped_ref[slot, k, at + 1 : at + 9],
                        )
                    )
                )
            values = (
                (single * state[1] - total[1]) + (real * state[3] + imag * state[2]),
                (total[0] - single * state[0]) + (imag * state[3] - real * state[2]),
                (total[3] - single * state[3]) + (real * state[1] - imag * state[0]),
                (single * state[2] - total[2]) - (real * state[0] + imag * state[1]),
            )
            for c in range(4):
                value = values[c]
                if target is None:
                    value = value * weights[4] + state[c] * weights[3]
                    for k in (2, 1):
                        value = value + terms[k][c, where, :] * weights[k]
                    terms[1][c, where, :] = value + terms[0][c, where, :]
                else:
                    target[c, where, :] = value

    block = 2 * STEP

    def leave(index, c):
        where = pl.ds(pl.multiple_of(index * (block * PLANE), 8), block * PLANE)
        return pltpu.make_async_copy(terms[1].at[c, where, :], out_ref.at[where, c, :], left.at[index, c])

    for source, target in zip(terms, terms[1:] + [None]):
        in_lanes(source, 0, 0)

        def body(index, carry, source=source, target=target):
            for slot in range(2):
                first = index * block + slot * STEP
                for p in range(STEP):
                    finish(source, target, first + p, p, slot)
                in_lanes(source, (first + STEP) & (NX - 1), 1 - slot)
            if target is None:
                for c in range(4):
                    leave(index, c).start()
            return carry

        lax.fori_loop(0, NX // block, body, 0)
    for index in range(NX // block):
        for c in range(4):
            leave(index, c).wait()


VMEM = pl.BlockSpec(memory_space=pltpu.VMEM)
ANY = pl.BlockSpec(memory_space=pl.ANY)
SMEM = pl.BlockSpec(memory_space=pltpu.SMEM)


def call(kernel, name, out_shapes, operands, scratch=(), in_specs=None, out_specs=None, limit=16):
    moved = sum(math.prod(o.shape) * 4 for o in (*out_shapes, *operands))
    return pl.pallas_call(
        kernel,
        name=name,
        out_shape=[jax.ShapeDtypeStruct(o.shape, o.dtype) for o in out_shapes],
        in_specs=in_specs or [VMEM] * len(operands),
        out_specs=out_specs or [VMEM] * len(out_shapes),
        scratch_shapes=[pltpu.VMEM(s, F32) if isinstance(s, tuple) else s for s in scratch],
        compiler_params=pltpu.CompilerParams(vmem_limit_bytes=limit * 1024 * 1024),
        cost_estimate=pl.CostEstimate(flops=0, bytes_accessed=moved, transcendentals=0),
    )(*operands)


def like(*shape):
    return jax.ShapeDtypeStruct(shape, F32)


def local(quasi, outer_field, coupling):
    sizes = {name: lax.axis_size(name) for name in AXES}
    devices = sizes["grp"] * sizes["wf"]
    waves = quasi.shape[0]
    scale = 1.0 / (waves * devices)
    bits = [("grp", 1 << k) for k in range(1, sizes["grp"].bit_length() - 1)]
    bits += [("wf", 1 << k) for k in range(sizes["wf"].bit_length() - 1)]
    first, second, third, rest = bits[0], bits[1], bits[2], bits[3:]
    straight = [first, second, third] + rest
    crossed = [second, first, third] + rest
    real_plan = Plan(sizes, (straight, crossed), devices)
    imag_plan = Plan(sizes, (crossed, straight), devices)
    mean_plan = Plan(sizes, ([third, first, second] + rest, [third, second, first] + rest), min(devices, NG))
    tables = {name: jnp.asarray(table) for name, table in transform_tables().items()}

    def halves(plan):
        return [like(plan.pieces // 2, ROWS // plan.pieces, LANES)] * 2

    state = quasi.reshape(waves, 4, ROWS, LANES).transpose(0, 2, 1, 3)
    outer_field = outer_field.reshape(ROWS, LANES)
    coupling = coupling.reshape(ROWS, LANES)

    real_own, real_other, imag_own, imag_other, psi = call(
        functools.partial(kappa_kernel, (real_plan, imag_plan), scale),
        "kappa", halves(real_plan) + halves(imag_plan) + [like(waves, 4, ROWS, LANES)], [state],
        [(ROWS, LANES)] * 2 + [pltpu.SemaphoreType.DMA((CHUNKS, waves, 4))], in_specs=[ANY],
    )
    mean_own, mean_other = call(
        functools.partial(density_kernel, mean_plan, scale),
        "density", halves(mean_plan), [psi, tables["forward_y"], tables["forward_z"]], [(ROWS, LANES)],
    )
    real = reduce_scatter(real_plan, real_own, real_other)
    imag = reduce_scatter(imag_plan, imag_own, imag_other)
    mean = reduce_scatter(mean_plan, mean_own, mean_other)
    (spectrum,) = call(
        functools.partial(coulomb_kernel, mean_plan),
        "coulomb", [like(*mean[0].shape)],
        [*mean, tables["even"], tables["odd"], tables["symbol_xz"], tables["symbol_y"]],
        in_specs=[VMEM] * 5 + [SMEM],
    )
    mean_parts = all_gather(mean_plan, spectrum)
    real_parts = all_gather(real_plan, real[0] + real[1])
    imag_parts = all_gather(imag_plan, imag[0] + imag[1])
    (mean_field,) = call(
        functools.partial(mean_kernel, mean_plan),
        "mean", [like(ROWS, LANES)],
        [*mean_parts, outer_field, tables["inverse_y"], tables["inverse_z"]], [(ROWS, LANES)],
    )

    evolved = []
    for wave in range(waves):
        evolved_rows, potentials = call(
            functools.partial(propagate_kernel, (real_plan, imag_plan)),
            "propagate",
            [like(ROWS, 4, LANES), like(3, NX // sizes["grp"], NG * NG // sizes["wf"])],
            [psi[wave : wave + 1], mean_field, coupling, tables["shift"], *real_parts, *imag_parts],
            [(ROWS, LANES)] * 3
            + [(2, 4 * STEP * PLANE, LANES), (2, 4 * STEP, PADDED, LANES)]
            + [(4, ROWS, LANES)] * 3
            + [pltpu.SemaphoreType.DMA((NX // (2 * STEP), 4))],
            out_specs=[ANY, VMEM],
            limit=32,
        )
        evolved.append(evolved_rows)
    evolved = jnp.stack(evolved) if waves > 1 else evolved[0][None]
    evolved = evolved.transpose(0, 2, 1, 3).reshape(quasi.shape)
    return (evolved, potentials)


def solution(mesh):
    placed = (P(AXES, None, None), P(), P())
    return jax.shard_map(
        local,
        mesh=mesh,
        in_specs=placed,
        out_specs=(P(AXES, None, None), P(None, "grp", "wf")),
        check_vma=False,
    )
```

time: 108 us -> 93.9 us (0.87)
  Pallas kernels: 47.8 us -> 34.3 us
  other arithmetic: 5.44 us -> 0.49 us
  waiting for transfers between devices: 11.4 us -> 16.2 us
    pallas_call x5, Pallas kernels: 47.8 us -> 34.3 us  [call(): pl.pallas_call(kernel, name=name, out_shape=[jax.ShapeDtypeStruct(o.shape...]
    ppermute x12, waiting for transfers between devices: 8.3 us -> 11.1 us  [all_gather(): parts = [whole, lax.ppermute(whole, AXES, plan.permutation(step))]]
    add x12, other arithmetic: 3.04 us -> 0.37 us  [reduce_scatter(): own, other = (own[:half] + received[:half], own[half:] + received[half:])]
    concatenate x9, other arithmetic: 2.38 us -> 0.1 us  [all_gather(): whole = parts[0] if len(parts) == 1 else jnp.concatenate(parts)]
    ppermute x15, waiting for transfers between devices: 3.11 us -> 5.12 us  [reduce_scatter(): received = lax.ppermute(other, AXES, plan.permutation(step))]
    unnamed x28 -> x24, local copies, waits for them, and re-layouts: 2.23 us -> 2.23 us
  transfers between devices with their start and end apart: 33 -> 33, of which waited for: 9 -> 9; matrix products, arithmetic and copies ran while one was open for 5% -> 1% of each run, Pallas kernels for 14% -> 10%
where the time goes in v3:
time: 93.9 us; the launch traced here: 93.8 us
  starting transfers between devices  39.6 us (42%)
  Pallas kernels  34.3 us (37%)
  waiting for transfers between devices  16.2 us (17%)
  local copies, waits for them, and re-layouts  2.23 us (2%)
    pallas_call x5, Pallas kernels, call(): pl.pallas_call(kernel, name=name, out_shape=[jax.ShapeDtypeStruct(o.shape...  34.3 us
    ppermute x15, starting transfers between devices, reduce_scatter(): received = lax.ppermute(other, AXES, plan.permutation(step))  22.4 us
    ppermute x12, starting transfers between devices, all_gather(): parts = [whole, lax.ppermute(whole, AXES, plan.permutation(step))]  16.2 us
    ppermute x12, waiting for transfers between devices, all_gather(): parts = [whole, lax.ppermute(whole, AXES, plan.permutation(step))]  11.1 us
    ppermute x15, waiting for transfers between devices, reduce_scatter(): received = lax.ppermute(other, AXES, plan.permutation(step))  5.12 us
    unnamed x24, local copies, waits for them, and re-layouts  2.23 us
  transfers between devices with their start and end apart: 33, of which 9 were waited for; matrix products, arithmetic and copies ran while one was open for 1% of the time, Pallas kernels for 10%

profile of v3, /device:TPU:0, one launch (start us, length us, event | category | flops | bytes accessed | tf_op | source)
XLA Modules:
  0.0 93.8 jit_solution(13109759264815349925)
XLA Ops:
  0.6 2.2 %copy-done = f32[1,4,262144]{2,1,0:T(4,128)S(1)} copy-done((f32[1,4,262144]{2,1,0:T(4,128)S(1)}, f32[1,4,262144]{2,1,0:T(4,128)}, u32[]{:S(2)}) %copy-start) | copy-done | bytes 4194328
  2.8 4.0 %kappa.1 = (f32[16,64,128]{2,1,0:T(8,128)S(1)}, f32[16,64,128]{2,1,0:T(8,128)S(1)}, f32[16,64,128]{2,1,0:T(8,128)S(1)}, f32[16,64,128]{2,1,0:T(8,128)S(1)}, f32[1,4,2048,128]{3,2,1,0:T(8,128)S(1)}) custom-call(f32[1,2048,4,128]{3,2,1,0:T(4,128)S(1)} %bitcast.10), custom_call_target="tpu_custom_call" | custom-call | bytes 10485760 | tf_op jit(solution)/shard_map/kappa/pallas_call | solution.py:446
  7.4 4.2 %density.1 = (f32[16,64,128]{2,1,0:T(8,128)S(1)}, f32[16,64,128]{2,1,0:T(8,128)S(1)}) custom-call(f32[1,4,2048,128]{3,2,1,0:T(8,128)S(1)} %get-tuple-element.11.psi_ref.refs_0_, bf16[2,256,256]{2,1,0:T(8,128)(2,1)S(1)} %copy-done.3, bf16[2,128,128]{2,1,0:T(8,128)(2,1)S(1)} %copy-done.6), custom_call_target="tpu_custom_call" | custom-call | bytes 5898240 | tf_op jit(solution)/shard_map/density/pallas_call | solution.py:446
  12.3 2.6 %collective-permute-start.12 = (f32[8,64,128]{2,1,0:T(8,128)S(1)}, f32[8,64,128]{2,1,0:T(8,128)S(1)}, u32[]{:S(2)}, u32[]{:S(2)}) collective-permute-start(f32[8,64,128]{2,1,0:T(8,128)S(1)} %get-tuple-element.23), channel_id=1, source_target_pairs={{0,16},{1,17},{2,18},{3,19},{4,20},{5,21},{6,22},{7,23},{8,9},{9,8... | collective-permute-start | bytes 786440 | tf_op jit(solution)/shard_map/ppermute | solution.py:129
  15.0 1.6 %collective-permute-start.23 = (f32[8,64,128]{2,1,0:T(8,128)S(1)}, f32[8,64,128]{2,1,0:T(8,128)S(1)}, u32[]{:S(2)}, u32[]{:S(2)}) collective-permute-start(f32[8,64,128]{2,1,0:T(8,128)S(1)} %get-tuple-element.21), channel_id=1, source_target_pairs={{0,1},{1,0},{2,3},{3,2},{4,5},{5,4},{6,7},{7,6},{8,24},{9,25},{10,... | collective-permute-start | bytes 786440 | tf_op jit(solution)/shard_map/ppermute | solution.py:129
  16.6 1.7 %collective-permute-start.1 = (f32[8,64,128]{2,1,0:T(8,128)S(1)}, f32[8,64,128]{2,1,0:T(8,128)S(1)}, u32[]{:S(2)}, u32[]{:S(2)}) collective-permute-start(f32[8,64,128]{2,1,0:T(8,128)S(1)} %get-tuple-element.25), channel_id=1, source_target_pairs={{0,2},{1,3},{2,0},{3,1},{4,6},{5,7},{6,4},{7,5},{8,10},{9,11},{10,... | collective-permute-start | bytes 786440 | tf_op jit(solution)/shard_map/ppermute | solution.py:129
  18.3 2.5 %collective-permute-done.12 = f32[8,64,128]{2,1,0:T(8,128)S(1)} collective-permute-done((f32[8,64,128]{2,1,0:T(8,128)S(1)}, f32[8,64,128]{2,1,0:T(8,128)S(1)}, u32[]{:S(2)}, u32[]{:S(2)}) %collective-permute-start.12) | collective-permute-done | bytes 262176 | tf_op jit(solution)/shard_map/ppermute | solution.py:129
  20.8 3.0 %collective-permute-start.13 = (f32[4,64,128]{2,1,0:T(8,128)S(1)}, f32[4,64,128]{2,1,0:T(8,128)S(1)}, u32[]{:S(2)}, u32[]{:S(2)}) collective-permute-start(f32[4,64,128]{2,1,0:T(8,128)S(1)} %get-tuple-element.29), channel_id=1, source_target_pairs={{0,1},{1,0},{2,3},{3,2},{4,5},{5,4},{6,7},{7,6},{8,24},{9,25},{10,... | collective-permute-start | bytes 393224 | tf_op jit(solution)/shard_map/ppermute | solution.py:129
  23.9 1.8 %collective-permute-start.24 = (f32[4,64,128]{2,1,0:T(8,128)S(1)}, f32[4,64,128]{2,1,0:T(8,128)S(1)}, u32[]{:S(2)}, u32[]{:S(2)}) collective-permute-start(f32[4,64,128]{2,1,0:T(8,128)S(1)} %get-tuple-element.27), channel_id=1, source_target_pairs={{0,16},{1,17},{2,18},{3,19},{4,20},{5,21},{6,22},{7,23},{8,9},{9,8... | collective-permute-start | bytes 393224 | tf_op jit(solution)/shard_map/ppermute | solution.py:129
  26.1 2.0 %collective-permute-done.13 = f32[4,64,128]{2,1,0:T(8,128)S(1)} collective-permute-done((f32[4,64,128]{2,1,0:T(8,128)S(1)}, f32[4,64,128]{2,1,0:T(8,128)S(1)}, u32[]{:S(2)}, u32[]{:S(2)}) %collective-permute-start.13) | collective-permute-done | bytes 131104 | tf_op jit(solution)/shard_map/ppermute | solution.py:129
  28.1 1.9 %collective-permute-start.14 = (f32[2,64,128]{2,1,0:T(8,128)S(1)}, f32[2,64,128]{2,1,0:T(8,128)S(1)}, u32[]{:S(2)}, u32[]{:S(2)}) collective-permute-start(f32[2,64,128]{2,1,0:T(8,128)S(1)} %get-tuple-element.35), channel_id=1, source_target_pairs={{0,2},{1,3},{2,0},{3,1},{4,6},{5,7},{6,4},{7,5},{8,10},{9,11},{10,... | collective-permute-start | bytes 196616 | tf_op jit(solution)/shard_map/ppermute | solution.py:129
  30.8 1.7 %collective-permute-start.3 = (f32[2,64,128]{2,1,0:T(8,128)S(1)}, f32[2,64,128]{2,1,0:T(8,128)S(1)}, u32[]{:S(2)}, u32[]{:S(2)}) collective-permute-start(f32[2,64,128]{2,1,0:T(8,128)S(1)} %get-tuple-element.37), channel_id=1, source_target_pairs={{0,1},{1,0},{2,3},{3,2},{4,5},{5,4},{6,7},{7,6},{8,24},{9,25},{10,... | collective-permute-start | bytes 196616 | tf_op jit(solution)/shard_map/ppermute | solution.py:129
  32.5 2.9 %collective-permute-start.15 = (f32[1,64,128]{2,1,0:T(8,128)S(1)}, f32[1,64,128]{2,1,0:T(8,128)S(1)}, u32[]{:S(2)}, u32[]{:S(2)}) collective-permute-start(f32[1,64,128]{2,1,0:T(8,128)S(1)} %slice_add_fusion.20), channel_id=1, source_target_pairs={{0,4},{1,5},{2,6},{3,7},{4,0},{5,1},{6,2},{7,3},{8,12},{9,13},{10,... | collective-permute-start | bytes 98312 | tf_op jit(solution)/shard_map/ppermute | solution.py:129
  35.4 1.9 %collective-permute-start.26 = (f32[1,64,128]{2,1,0:T(8,128)S(1)}, f32[1,64,128]{2,1,0:T(8,128)S(1)}, u32[]{:S(2)}, u32[]{:S(2)}) collective-permute-start(f32[1,64,128]{2,1,0:T(8,128)S(1)} %slice_add_fusion.18), channel_id=1, source_target_pairs={{0,4},{1,5},{2,6},{3,7},{4,0},{5,1},{6,2},{7,3},{8,12},{9,13},{10,... | collective-permute-start | bytes 98312 | tf_op jit(solution)/shard_map/ppermute | solution.py:129
  38.5 2.1 %collective-permute-start.16 = (f32[1,64,128]{2,1,0:T(8,128)S(1)}, f32[1,64,128]{2,1,0:T(8,128)S(1)}, u32[]{:S(2)}, u32[]{:S(2)}) collective-permute-start(f32[1,64,128]{2,1,0:T(8,128)S(1)} %fusion.1), channel_id=1, source_target_pairs={{0,4},{1,5},{2,6},{3,7},{4,0},{5,1},{6,2},{7,3},{8,12},{9,13},{10,... | collective-permute-start | bytes 98312 | tf_op jit(solution)/shard_map/ppermute | solution.py:145
  40.5 1.6 %collective-permute-start.27 = (f32[1,64,128]{2,1,0:T(8,128)S(1)}, f32[1,64,128]{2,1,0:T(8,128)S(1)}, u32[]{:S(2)}, u32[]{:S(2)}) collective-permute-start(f32[1,64,128]{2,1,0:T(8,128)S(1)} %fusion), channel_id=1, source_target_pairs={{0,4},{1,5},{2,6},{3,7},{4,0},{5,1},{6,2},{7,3},{8,12},{9,13},{10,... | collective-permute-start | bytes 98312 | tf_op jit(solution)/shard_map/ppermute | solution.py:145
  44.8 2.5 %collective-permute-start.17 = (f32[2,64,128]{2,1,0:T(8,128)S(1)}, f32[2,64,128]{2,1,0:T(8,128)S(1)}, u32[]{:S(2)}, u32[]{:S(2)}) collective-permute-start(f32[2,64,128]{2,1,0:T(8,128)S(1)} %pad_maximum_fusion.7), channel_id=1, source_target_pairs={{0,2},{1,3},{2,0},{3,1},{4,6},{5,7},{6,4},{7,5},{8,10},{9,11},{10,... | collective-permute-start | bytes 196616 | tf_op jit(solution)/shard_map/ppermute | solution.py:145
  48.8 1.8 %collective-permute-start.6 = (f32[2,64,128]{2,1,0:T(8,128)S(1)}, f32[2,64,128]{2,1,0:T(8,128)S(1)}, u32[]{:S(2)}, u32[]{:S(2)}) collective-permute-start(f32[2,64,128]{2,1,0:T(8,128)S(1)} %pad_maximum_fusion.6), channel_id=1, source_target_pairs={{0,1},{1,0},{2,3},{3,2},{4,5},{5,4},{6,7},{7,6},{8,24},{9,25},{10,... | collective-permute-start | bytes 196616 | tf_op jit(solution)/shard_map/ppermute | solution.py:145
  51.4 2.3 %collective-permute-done.6 = f32[2,64,128]{2,1,0:T(8,128)S(1)} collective-permute-done((f32[2,64,128]{2,1,0:T(8,128)S(1)}, f32[2,64,128]{2,1,0:T(8,128)S(1)}, u32[]{:S(2)}, u32[]{:S(2)}) %collective-permute-start.6) | collective-permute-done | bytes 65568 | tf_op jit(solution)/shard_map/ppermute | solution.py:145
  59.8 2.0 %collective-permute-start.8 = (f32[8,64,128]{2,1,0:T(8,128)S(1)}, f32[8,64,128]{2,1,0:T(8,128)S(1)}, u32[]{:S(2)}, u32[]{:S(2)}) collective-permute-start(f32[8,64,128]{2,1,0:T(8,128)S(1)} %pad_maximum_fusion.refs_0_), channel_id=1, source_target_pairs={{0,2},{1,3},{2,0},{3,1},{4,6},{5,7},{6,4},{7,5},{8,10},{9,11},{10,... | collective-permute-start | bytes 786440 | tf_op jit(solution)/shard_map/ppermute | solution.py:145
  62.4 3.9 %collective-permute-done.8.refs_1_ = f32[8,64,128]{2,1,0:T(8,128)S(1)} collective-permute-done((f32[8,64,128]{2,1,0:T(8,128)S(1)}, f32[8,64,128]{2,1,0:T(8,128)S(1)}, u32[]{:S(2)}, u32[]{:S(2)}) %collective-permute-start.8) | collective-permute-done | bytes 262176 | tf_op jit(solution)/shard_map/ppermute | solution.py:145
  66.8 1.5 %collective-permute-done.30.refs_9_ = f32[8,64,128]{2,1,0:T(8,128)S(1)} collective-permute-done((f32[8,64,128]{2,1,0:T(8,128)S(1)}, f32[8,64,128]{2,1,0:T(8,128)S(1)}, u32[]{:S(2)}, u32[]{:S(2)}) %collective-permute-start.30) | collective-permute-done | bytes 262176 | tf_op jit(solution)/shard_map/ppermute | solution.py:145
  68.8 3.7 %mean.1.refs_1_ = f32[2048,128]{1,0:T(8,128)S(1)} custom-call(f32[8,64,128]{2,1,0:T(8,128)S(1)} %pad_maximum_fusion.refs_0_, f32[8,64,128]{2,1,0:T(8,128)S(1)} %collective-permute-done.8.refs_1_, f32[8,64,128]{2,1,0:T(8,128)S(1)} %collective-permute-done.9.refs_2_, f32[8,64,128]{2,1,0:T(8,128)S(1)} %collective-permute-done.10.refs_3_, ...), custom_call_target="tpu_custom_call" | custom-call | bytes 3801088 | tf_op jit(solution)/shard_map/mean/pallas_call | solution.py:446
  72.5 21.3 %propagate.1 = (f32[2048,4,128]{2,1,0:T(4,128)}, f32[3,16,512]{2,1,0:T(8,128)}) custom-call(f32[1,4,2048,128]{3,2,1,0:T(8,128)S(1)} %get-tuple-element.11.psi_ref.refs_0_, f32[2048,128]{1,0:T(8,128)S(1)} %mean.1.refs_1_, f32[2048,128]{1,0:T(8,128)S(1)} %bitcast.12, bf16[256,256]{1,0:T(8,128)(2,1)S(1)} %copy-done.5, ...), custom_call_target="tpu_custom_call" | custom-call | bytes 12943360 | tf_op jit(solution)/shard_map/propagate/pallas_call | solution.py:446
  (94 shorter events, 16.6 us)
Async XLA Ops:
  6.8 5.4 %collective-permute-start.11 = (f32[16,64,128]{2,1,0:T(8,128)S(1)}, f32[16,64,128]{2,1,0:T(8,128)S(1)}, u32[]{:S(2)}, u32[]{:S(2)}) collective-permute-start(f32[16,64,128]{2,1,0:T(8,128)S(1)} %get-tuple-element.15), channel_id=1, source_target_pairs={{0,8},{1,9},{2,10},{3,11},{4,12},{5,13},{6,14},{7,15},{8,0},{9,1},... | collective-permute-start | bytes 1572872 | tf_op jit(solution)/shard_map/ppermute | solution.py:129
  7.4 7.5 %collective-permute-start.22 = (f32[16,64,128]{2,1,0:T(8,128)S(1)}, f32[16,64,128]{2,1,0:T(8,128)S(1)}, u32[]{:S(2)}, u32[]{:S(2)}) collective-permute-start(f32[16,64,128]{2,1,0:T(8,128)S(1)} %get-tuple-element.17), channel_id=1, source_target_pairs={{0,8},{1,9},{2,10},{3,11},{4,12},{5,13},{6,14},{7,15},{8,0},{9,1},... | collective-permute-start | bytes 1572872 | tf_op jit(solution)/shard_map/ppermute | solution.py:129
  12.3 8.5 %collective-permute-start.12 = (f32[8,64,128]{2,1,0:T(8,128)S(1)}, f32[8,64,128]{2,1,0:T(8,128)S(1)}, u32[]{:S(2)}, u32[]{:S(2)}) collective-permute-start(f32[8,64,128]{2,1,0:T(8,128)S(1)} %get-tuple-element.23), channel_id=1, source_target_pairs={{0,16},{1,17},{2,18},{3,19},{4,20},{5,21},{6,22},{7,23},{8,9},{9,8... | collective-permute-start | bytes 786440 | tf_op jit(solution)/shard_map/ppermute | solution.py:129
  15.0 8.9 %collective-permute-start.23 = (f32[8,64,128]{2,1,0:T(8,128)S(1)}, f32[8,64,128]{2,1,0:T(8,128)S(1)}, u32[]{:S(2)}, u32[]{:S(2)}) collective-permute-start(f32[8,64,128]{2,1,0:T(8,128)S(1)} %get-tuple-element.21), channel_id=1, source_target_pairs={{0,1},{1,0},{2,3},{3,2},{4,5},{5,4},{6,7},{7,6},{8,24},{9,25},{10,... | collective-permute-start | bytes 786440 | tf_op jit(solution)/shard_map/ppermute | solution.py:129
  16.6 9.0 %collective-permute-start.1 = (f32[8,64,128]{2,1,0:T(8,128)S(1)}, f32[8,64,128]{2,1,0:T(8,128)S(1)}, u32[]{:S(2)}, u32[]{:S(2)}) collective-permute-start(f32[8,64,128]{2,1,0:T(8,128)S(1)} %get-tuple-element.25), channel_id=1, source_target_pairs={{0,2},{1,3},{2,0},{3,1},{4,6},{5,7},{6,4},{7,5},{8,10},{9,11},{10,... | collective-permute-start | bytes 786440 | tf_op jit(solution)/shard_map/ppermute | solution.py:129
  20.8 7.3 %collective-permute-start.13 = (f32[4,64,128]{2,1,0:T(8,128)S(1)}, f32[4,64,128]{2,1,0:T(8,128)S(1)}, u32[]{:S(2)}, u32[]{:S(2)}) collective-permute-start(f32[4,64,128]{2,1,0:T(8,128)S(1)} %get-tuple-element.29), channel_id=1, source_target_pairs={{0,1},{1,0},{2,3},{3,2},{4,5},{5,4},{6,7},{7,6},{8,24},{9,25},{10,... | collective-permute-start | bytes 393224 | tf_op jit(solution)/shard_map/ppermute | solution.py:129
  23.9 6.2 %collective-permute-start.24 = (f32[4,64,128]{2,1,0:T(8,128)S(1)}, f32[4,64,128]{2,1,0:T(8,128)S(1)}, u32[]{:S(2)}, u32[]{:S(2)}) collective-permute-start(f32[4,64,128]{2,1,0:T(8,128)S(1)} %get-tuple-element.27), channel_id=1, source_target_pairs={{0,16},{1,17},{2,18},{3,19},{4,20},{5,21},{6,22},{7,23},{8,9},{9,8... | collective-permute-start | bytes 393224 | tf_op jit(solution)/shard_map/ppermute | solution.py:129
  30.1 5.3 %collective-permute-start.25 = (f32[2,64,128]{2,1,0:T(8,128)S(1)}, f32[2,64,128]{2,1,0:T(8,128)S(1)}, u32[]{:S(2)}, u32[]{:S(2)}) collective-permute-start(f32[2,64,128]{2,1,0:T(8,128)S(1)} %get-tuple-element.33), channel_id=1, source_target_pairs={{0,2},{1,3},{2,0},{3,1},{4,6},{5,7},{6,4},{7,5},{8,10},{9,11},{10,... | collective-permute-start | bytes 196616 | tf_op jit(solution)/shard_map/ppermute | solution.py:129
  30.8 6.4 %collective-permute-start.3 = (f32[2,64,128]{2,1,0:T(8,128)S(1)}, f32[2,64,128]{2,1,0:T(8,128)S(1)}, u32[]{:S(2)}, u32[]{:S(2)}) collective-permute-start(f32[2,64,128]{2,1,0:T(8,128)S(1)} %get-tuple-element.37), channel_id=1, source_target_pairs={{0,1},{1,0},{2,3},{3,2},{4,5},{5,4},{6,7},{7,6},{8,24},{9,25},{10,... | collective-permute-start | bytes 196616 | tf_op jit(solution)/shard_map/ppermute | solution.py:129
  32.5 6.0 %collective-permute-start.15 = (f32[1,64,128]{2,1,0:T(8,128)S(1)}, f32[1,64,128]{2,1,0:T(8,128)S(1)}, u32[]{:S(2)}, u32[]{:S(2)}) collective-permute-start(f32[1,64,128]{2,1,0:T(8,128)S(1)} %slice_add_fusion.20), channel_id=1, source_target_pairs={{0,4},{1,5},{2,6},{3,7},{4,0},{5,1},{6,2},{7,3},{8,12},{9,13},{10,... | collective-permute-start | bytes 98312 | tf_op jit(solution)/shard_map/ppermute | solution.py:129
  37.2 5.5 %collective-permute-start.4 = (f32[1,64,128]{2,1,0:T(8,128)S(1)}, f32[1,64,128]{2,1,0:T(8,128)S(1)}, u32[]{:S(2)}, u32[]{:S(2)}) collective-permute-start(f32[1,64,128]{2,1,0:T(8,128)S(1)} %get-tuple-element.38), channel_id=1, source_target_pairs={{0,4},{1,5},{2,6},{3,7},{4,0},{5,1},{6,2},{7,3},{8,12},{9,13},{10,... | collective-permute-start | bytes 98312 | tf_op jit(solution)/shard_map/ppermute | solution.py:129
  38.5 6.3 %collective-permute-start.16 = (f32[1,64,128]{2,1,0:T(8,128)S(1)}, f32[1,64,128]{2,1,0:T(8,128)S(1)}, u32[]{:S(2)}, u32[]{:S(2)}) collective-permute-start(f32[1,64,128]{2,1,0:T(8,128)S(1)} %fusion.1), channel_id=1, source_target_pairs={{0,4},{1,5},{2,6},{3,7},{4,0},{5,1},{6,2},{7,3},{8,12},{9,13},{10,... | collective-permute-start | bytes 98312 | tf_op jit(solution)/shard_map/ppermute | solution.py:145
  40.5 6.8 %collective-permute-start.27 = (f32[1,64,128]{2,1,0:T(8,128)S(1)}, f32[1,64,128]{2,1,0:T(8,128)S(1)}, u32[]{:S(2)}, u32[]{:S(2)}) collective-permute-start(f32[1,64,128]{2,1,0:T(8,128)S(1)} %fusion), channel_id=1, source_target_pairs={{0,4},{1,5},{2,6},{3,7},{4,0},{5,1},{6,2},{7,3},{8,12},{9,13},{10,... | collective-permute-start | bytes 98312 | tf_op jit(solution)/shard_map/ppermute | solution.py:145
  44.8 5.8 %collective-permute-start.17 = (f32[2,64,128]{2,1,0:T(8,128)S(1)}, f32[2,64,128]{2,1,0:T(8,128)S(1)}, u32[]{:S(2)}, u32[]{:S(2)}) collective-permute-start(f32[2,64,128]{2,1,0:T(8,128)S(1)} %pad_maximum_fusion.7), channel_id=1, source_target_pairs={{0,2},{1,3},{2,0},{3,1},{4,6},{5,7},{6,4},{7,5},{8,10},{9,11},{10,... | collective-permute-start | bytes 196616 | tf_op jit(solution)/shard_map/ppermute | solution.py:145
  47.3 7.6 %collective-permute-start.28 = (f32[2,64,128]{2,1,0:T(8,128)S(1)}, f32[2,64,128]{2,1,0:T(8,128)S(1)}, u32[]{:S(2)}, u32[]{:S(2)}) collective-permute-start(f32[2,64,128]{2,1,0:T(8,128)S(1)} %pad_maximum_fusion.8), channel_id=1, source_target_pairs={{0,2},{1,3},{2,0},{3,1},{4,6},{5,7},{6,4},{7,5},{8,10},{9,11},{10,... | collective-permute-start | bytes 196616 | tf_op jit(solution)/shard_map/ppermute | solution.py:145
  50.6 6.4 %collective-permute-start.18 = (f32[4,64,128]{2,1,0:T(8,128)S(1)}, f32[4,64,128]{2,1,0:T(8,128)S(1)}, u32[]{:S(2)}, u32[]{:S(2)}) collective-permute-start(f32[4,64,128]{2,1,0:T(8,128)S(1)} %pad_maximum_fusion.4), channel_id=1, source_target_pairs={{0,1},{1,0},{2,3},{3,2},{4,5},{5,4},{6,7},{7,6},{8,24},{9,25},{10,... | collective-permute-start | bytes 393224 | tf_op jit(solution)/shard_map/ppermute | solution.py:145
  53.7 6.0 %collective-permute-start.7 = (f32[4,64,128]{2,1,0:T(8,128)S(1)}, f32[4,64,128]{2,1,0:T(8,128)S(1)}, u32[]{:S(2)}, u32[]{:S(2)}) collective-permute-start(f32[4,64,128]{2,1,0:T(8,128)S(1)} %pad_maximum_fusion.3), channel_id=1, source_target_pairs={{0,16},{1,17},{2,18},{3,19},{4,20},{5,21},{6,22},{7,23},{8,9},{9,8... | collective-permute-start | bytes 393224 | tf_op jit(solution)/shard_map/ppermute | solution.py:145
  54.9 6.9 %collective-permute-start.29 = (f32[4,64,128]{2,1,0:T(8,128)S(1)}, f32[4,64,128]{2,1,0:T(8,128)S(1)}, u32[]{:S(2)}, u32[]{:S(2)}) collective-permute-start(f32[4,64,128]{2,1,0:T(8,128)S(1)} %pad_maximum_fusion.5), channel_id=1, source_target_pairs={{0,16},{1,17},{2,18},{3,19},{4,20},{5,21},{6,22},{7,23},{8,9},{9,8... | collective-permute-start | bytes 393224 | tf_op jit(solution)/shard_map/ppermute | solution.py:145
  57.0 9.7 %collective-permute-start.19 = (f32[8,64,128]{2,1,0:T(8,128)S(1)}, f32[8,64,128]{2,1,0:T(8,128)S(1)}, u32[]{:S(2)}, u32[]{:S(2)}) collective-permute-start(f32[8,64,128]{2,1,0:T(8,128)S(1)} %pad_maximum_fusion.1.refs_4_), channel_id=1, source_target_pairs={{0,16},{1,17},{2,18},{3,19},{4,20},{5,21},{6,22},{7,23},{8,9},{9,8... | collective-permute-start | bytes 786440 | tf_op jit(solution)/shard_map/ppermute | solution.py:145
  59.8 6.4 %collective-permute-start.8 = (f32[8,64,128]{2,1,0:T(8,128)S(1)}, f32[8,64,128]{2,1,0:T(8,128)S(1)}, u32[]{:S(2)}, u32[]{:S(2)}) collective-permute-start(f32[8,64,128]{2,1,0:T(8,128)S(1)} %pad_maximum_fusion.refs_0_), channel_id=1, source_target_pairs={{0,2},{1,3},{2,0},{3,1},{4,6},{5,7},{6,4},{7,5},{8,10},{9,11},{10,... | collective-permute-start | bytes 786440 | tf_op jit(solution)/shard_map/ppermute | solution.py:145
  61.8 6.4 %collective-permute-start.30 = (f32[8,64,128]{2,1,0:T(8,128)S(1)}, f32[8,64,128]{2,1,0:T(8,128)S(1)}, u32[]{:S(2)}, u32[]{:S(2)}) collective-permute-start(f32[8,64,128]{2,1,0:T(8,128)S(1)} %pad_maximum_fusion.2.refs_8_), channel_id=1, source_target_pairs={{0,1},{1,0},{2,3},{3,2},{4,5},{5,4},{6,7},{7,6},{8,24},{9,25},{10,... | collective-permute-start | bytes 786440 | tf_op jit(solution)/shard_map/ppermute | solution.py:145
  62.4 5.9 %collective-permute-start.9 = (f32[8,64,128]{2,1,0:T(8,128)S(1)}, f32[8,64,128]{2,1,0:T(8,128)S(1)}, u32[]{:S(2)}, u32[]{:S(2)}) collective-permute-start(f32[8,64,128]{2,1,0:T(8,128)S(1)} %pad_maximum_fusion.refs_0_), channel_id=1, source_target_pairs={{0,8},{1,9},{2,10},{3,11},{4,12},{5,13},{6,14},{7,15},{8,0},{9,1},... | collective-permute-start | bytes 786440 | tf_op jit(solution)/shard_map/ppermute | solution.py:146
  66.2 6.2 %collective-permute-start.20 = (f32[8,64,128]{2,1,0:T(8,128)S(1)}, f32[8,64,128]{2,1,0:T(8,128)S(1)}, u32[]{:S(2)}, u32[]{:S(2)}) collective-permute-start(f32[8,64,128]{2,1,0:T(8,128)S(1)} %pad_maximum_fusion.1.refs_4_), channel_id=1, source_target_pairs={{0,8},{1,9},{2,10},{3,11},{4,12},{5,13},{6,14},{7,15},{8,0},{9,1},... | collective-permute-start | bytes 786440 | tf_op jit(solution)/shard_map/ppermute | solution.py:146
  66.8 5.7 %collective-permute-start.31 = (f32[8,64,128]{2,1,0:T(8,128)S(1)}, f32[8,64,128]{2,1,0:T(8,128)S(1)}, u32[]{:S(2)}, u32[]{:S(2)}) collective-permute-start(f32[8,64,128]{2,1,0:T(8,128)S(1)} %pad_maximum_fusion.2.refs_8_), channel_id=1, source_target_pairs={{0,8},{1,9},{2,10},{3,11},{4,12},{5,13},{6,14},{7,15},{8,0},{9,1},... | collective-permute-start | bytes 786440 | tf_op jit(solution)/shard_map/ppermute | solution.py:146
  (21 other events, 424.2 us)
